TPU v7x, 768 devices: a whole 4x8x12 slice. The times are simulated.
768 devices in a mesh: wide: 48 (over y_hi, z, core), tensor: 16 (over y_lo, x).
Axes of the slice: x: 4, y: 8 (y_hi: 2, y_lo: 4; y = y_hi * 4 + y_lo), z: 12, core: 2. Of those that a mesh axis runs over, the one named last changes fastest.
Arguments:
- hidden: bfloat16 [73728, 3072], P('wide', 'tensor'), may hold values from -6 to 6
- modulation: float32 [2, 3072], P(None, 'tensor'), may hold values from -3 to 3
- final_weight: bfloat16 [3072, 64], P('tensor'), may hold values from -0.109375 to 0.109375
- noisy: float32 [73728, 64], P('wide'), may hold values from -6 to 6
- step_index: int32 [1], replicated, may hold values from 1 to 28
- slab_table: int32 [1152], P('wide'), may hold values from 0 to 47, as said below
- conv_in_weight: bfloat16 [144, 512], P(None, 'tensor'), may hold values from -0.5 to 0.5
- conv_in_bias: float32 [512], P('tensor'), may hold values from -3 to 3
- conv1_weight: bfloat16 [9, 512, 512], replicated, may hold values from -0.09375 to 0.09375
- conv1_bias: float32 [512], replicated, may hold values from -3 to 3
Outputs:
- decoder_features: bfloat16 [2304, 512, 128], P('wide', 'tensor')
- residual_branch: bfloat16 [2304, 512, 128], P('wide', 'tensor')
Inputs may be any that keep to these rules, and one draw needn't show every extreme that they name: There are 24 distinct offsets o_j, one per local row j, with slab_table[w * 24 + j] = (w - o_j) modulo the number of wide devices: each slab receives each local row index from exactly one wide device, and the rows of one device go to distinct slabs. One of the offsets is half the number of wide devices (rounded down).
All inputs are finite; a program needn't handle non-finite values.
Results may differ from a plain program's by a relative error of at most 0.012.
Values may be sent and summed in bfloat16 or wider, within the bound.
No kernel may reach another device: no remote copies, remote signals or barrier semaphores. Data moves between devices by JAX's collectives and lax.ppermute only.
A program may use at most 64 MiB of HBM per device.

v0:
```python
import jax
import jax.numpy as jnp
from jax import lax
from jax.sharding import PartitionSpec as P

D = 3072
LC = 16
GRID = 64
STEPS = 28


shift_value = 3.0
norm_eps = 1e-06


def padded_2(value, sides, width):
    for axis, dim in sides:
        count, length = (lax.axis_size(axis), value.shape[dim])
        up = [(i, (i + 1) % count) for i in range(count - 1)]
        down = [(j, i) for i, j in up]
        last = lax.slice_in_dim(value, length - width, length, axis=dim)
        first = lax.slice_in_dim(value, 0, width, axis=dim)
        before = lax.ppermute(last, axis, up)
        after = lax.ppermute(first, axis, down)
        value = jnp.concatenate([before, value, after], axis=dim)
    return value


def edge_masks(first_row, count, height):
    global_rows = first_row + jnp.arange(count, dtype=jnp.int32)
    upper = (global_rows % height != 0).astype(jnp.float32)
    lower = (global_rows % height != height - 1).astype(jnp.float32)
    return (upper, jnp.ones_like(upper), lower)


def conv_input_rows(latent, weight, bias, first_row, count, channels):
    width = latent.shape[1] // channels
    planes = latent.reshape(latent.shape[0], width, channels)
    padded = jnp.pad(planes, ((0, 0), (1, 1), (0, 0)))
    masks = edge_masks(first_row, count, width)
    pieces = []
    for row_off in range(3):
        keep = masks[row_off].astype(jnp.bfloat16)[:, None, None]
        for col_off in range(3):
            pieces.append(padded[row_off : row_off + count, col_off : col_off + width, :] * keep)
    patches = jnp.concatenate(pieces, axis=-1)
    return jnp.einsum("rwk,ko->rwo", patches, weight, preferred_element_type=jnp.float32) + bias


def conv_three(total, inputs, weights, first_row, count):
    width = inputs.shape[2]
    padded = jnp.pad(inputs, ((0, 0), (0, 0), (1, 1)))
    masks = edge_masks(first_row, count, width)
    for row_off in range(3):
        keep = masks[row_off][:, None, None]
        for col_off in range(3):
            window = padded[row_off : row_off + count, :, col_off : col_off + width]
            term = jnp.einsum(
                "rkw,ko->row",
                window,
                weights[3 * row_off + col_off],
                preferred_element_type=jnp.float32,
            )
            total = total + keep * term
    return total


def shards(
    hidden,
    modulation,
    final_weight,
    noisy,
    step_index,
    slab_table,
    conv_in_weight,
    conv_in_bias,
    conv1_weight,
    conv1_bias,
):
    feats = hidden.astype(jnp.float32)
    weight_f = final_weight.astype(jnp.float32)
    width_all = D
    first_sum, square_sum = lax.psum(
        (jnp.sum(feats, axis=-1), jnp.sum(feats * feats, axis=-1)), "tensor"
    )
    mean = first_sum / width_all
    rstd = 1.0 / jnp.sqrt(square_sum / width_all - mean * mean + norm_eps)
    normed = (feats - mean[:, None]) * rstd[:, None] * (1.0 + modulation[1]) + modulation[0]
    partial_proj = jnp.dot(normed, weight_f, precision=lax.Precision.HIGHEST)
    velocity = lax.psum(partial_proj, "tensor")
    frac = step_index[0].astype(jnp.float32) / STEPS
    sigma = shift_value * frac / (1.0 + (shift_value - 1.0) * frac)
    clean = (noisy - sigma * velocity).astype(jnp.bfloat16)
    rows_here = slab_table.shape[0]
    token_rows = clean.reshape(rows_here, -1)
    slabs = lax.axis_size("wide")
    slab_here = lax.axis_index("wide")
    slab_ids = jnp.arange(slabs, dtype=jnp.int32)
    outgoing = (slab_ids[:, None] == slab_table[None, :]).astype(jnp.bfloat16)
    sendbuf = jnp.dot(outgoing, token_rows, preferred_element_type=jnp.float32).astype(jnp.bfloat16)
    received = lax.all_to_all(sendbuf, "wide", split_axis=0, concat_axis=0, tiled=True)
    source = (2 * slab_here - slab_table) % slabs
    incoming = (source[:, None] == slab_ids[None, :]).astype(jnp.bfloat16)
    slab_rows = jnp.dot(incoming, received, preferred_element_type=jnp.float32).astype(jnp.bfloat16)
    grid_side = GRID
    channels = LC
    pixel_rows = (
        slab_rows.reshape(rows_here, grid_side, 2, 2, channels)
        .transpose(0, 2, 1, 3, 4)
        .reshape(2 * rows_here, 4 * grid_side * channels // 2)
    )
    depth = 2
    latent = padded_2(pixel_rows, (("wide", 0),), depth)
    slab_height = 2 * rows_here
    conv_rows = slab_height + 2 * (depth - 1)
    first_conv = slab_here * slab_height - (depth - 1)
    first = conv_input_rows(latent, conv_in_weight, conv_in_bias, first_conv, conv_rows, channels)
    features = first.astype(jnp.bfloat16).transpose(0, 2, 1)
    activated = jax.nn.silu(features.astype(jnp.float32)).astype(jnp.bfloat16)
    decoder_features = features[depth - 1 : depth - 1 + slab_height]
    local_out = conv_in_weight.shape[1]
    tensor_here = lax.axis_index("tensor")
    pixel_width = activated.shape[2]
    columns = lax.dynamic_slice_in_dim(conv1_weight, tensor_here * local_out, local_out, 2)
    bias_part = lax.dynamic_slice_in_dim(conv1_bias, tensor_here * local_out, local_out, 0)
    first_out = slab_here * slab_height
    gathered = lax.all_gather(activated, "tensor", axis=1, tiled=True)
    start_total = jnp.zeros((slab_height, local_out, pixel_width), jnp.float32)
    summed = conv_three(start_total, gathered, columns, first_out, slab_height)
    residual_branch = (summed + bias_part[None, :, None]).astype(jnp.bfloat16)
    return (decoder_features, residual_branch)


def solution(mesh):
    return jax.shard_map(
        shards,
        mesh=mesh,
        in_specs=(
            P("wide", "tensor"),
            P(None, "tensor"),
            P("tensor", None),
            P("wide", None),
            P(),
            P("wide"),
            P(None, "tensor"),
            P("tensor"),
            P(),
            P(),
        ),
        out_specs=(P("wide", "tensor", None), P("wide", "tensor", None)),
        check_vma=False,
    )
```

profile of v0, /device:TPU:1, one launch (start us, length us, event | category | flops | bytes accessed | tf_op | source)
XLA Modules:
  0.0 444.3 jit_solution(11848395175837721234)
XLA Ops:
  7.2 1.2 convert_reduce_fusion
  8.5 0.8 slice_add_fusion
  9.2 66.6 %all-reduce.2 = (f32[1536]{0:T(1024)S(1)}, f32[1536]{0:T(1024)S(1)}) all-reduce(f32[1536]{0:T(1024)S(1)} %get-tuple-element.3, f32[1536]{0:T(1024)S(1)} %get-tuple-element.2), channel_id=1, replica_groups=mesh['wide'=48,'tensor'=16] {'tensor'}, use_global_device_ids=true, to_apply=%region_3.0 | all-reduce | flops 3072 | bytes 24576 | tf_op jit(solution)/shard_map/psum | solution.py:83
  75.8 2.6 fusion.35
  79.1 176.4 %all-reduce.5.cloned.1.call-done = f32[1536,64]{0,1:T(8,128)} async-done(((f32[1536,64]{0,1:T(8,128)}), f32[1536,64]{0,1:T(8,128)}) %all-reduce.5.cloned.1.call-update) | async-done | bytes 393232 | tf_op jit(solution)/shard_map/psum | solution.py:90
  255.6 1.2 subtract_convert_fusion
  257.6 0.5 broadcast.159
  258.1 0.9 reduce
  259.0 1.0 reshape.90
  260.0 25.2 %all-to-all-start = ((bf16[48,2,2048]{2,1,0:T(2,128)(2,1)}), bf16[48,2,2048]{2,1,0:T(2,128)(2,1)S(1)}, u32[]{:S(2)}, u32[]{:S(2)}) async-start(bf16[48,2,2048]{2,1,0:T(2,128)(2,1)} %reshape.90), calls=%async_computation | async-start | bytes 786432 | tf_op jit(solution)/shard_map/all_to_all | solution.py:101
  285.4 21.6 %all-to-all-done = bf16[48,2,2048]{2,1,0:T(2,128)(2,1)S(1)} async-done(((bf16[48,2,2048]{2,1,0:T(2,128)(2,1)}), bf16[48,2,2048]{2,1,0:T(2,128)(2,1)S(1)}, u32[]{:S(2)}, u32[]{:S(2)}) %all-to-all-start) | async-done | bytes 393248 | tf_op jit(solution)/shard_map/all_to_all | solution.py:101
  307.0 0.4 reshape.91
  307.4 0.5 convolution_convert_fusion.1
  307.9 1.3 reshape.79
  309.5 3.4 collective-permute-start
  313.1 1.9 collective-permute-start.1
  315.0 1.7 copy.42
  316.7 0.8 copy.45
  319.8 1.2 fusion.41
  321.0 0.8 dynamic_slice.7
  321.8 0.8 slice.141
  322.6 86.1 %all-gather.2.cloned.1.call-done = bf16[50,512,128]{2,1,0:T(8,128)(2,1)} async-done(((bf16[50,32,128]{2,1,0:T(8,128)(2,1)}), bf16[50,512,128]{2,1,0:T(8,128)(2,1)}) %all-gather.2.cloned.1.call-update) | async-done | bytes 6553616 | tf_op jit(solution)/shard_map/all_gather | solution.py:127
  408.7 4.3 fusion.4
  413.0 0.4 copy-done.1
  413.4 3.0 fusion.24
  416.5 2.2 fusion.2
  418.7 3.0 fusion.23
  421.6 3.2 fusion.21
  424.8 3.0 fusion.19
  427.9 2.4 fusion.26
  430.3 3.1 fusion.18
  433.4 4.1 fusion.31
  (42 shorter events, 3.7 us)
Async XLA Ops:
  7.2 68.7 %copy-start = (bf16[192,64]{0,1:T(8,128)(2,1)S(1)}, bf16[192,64]{0,1:T(8,128)(2,1)}, u32[]{:S(2)}) copy-start(bf16[192,64]{0,1:T(8,128)(2,1)} %param.12) | copy-start | bytes 73732
  7.2 250.2 %copy-start.2 = (s32[24]{0:T(128)S(1)}, s32[24]{0:T(128)}, u32[]{:S(2)}) copy-start(s32[24]{0:T(128)} %param.15) | copy-start | bytes 292
  7.2 248.4 %all-reduce.5.cloned.1.call-start = ((), (), s32[]{:S(2)}) async-start(), calls=%async_computation.1 | async-start | bytes 786432 | tf_op jit(solution)/shard_map/psum | solution.py:90
  260.0 46.9 %all-to-all-start = ((bf16[48,2,2048]{2,1,0:T(2,128)(2,1)}), bf16[48,2,2048]{2,1,0:T(2,128)(2,1)S(1)}, u32[]{:S(2)}, u32[]{:S(2)}) async-start(bf16[48,2,2048]{2,1,0:T(2,128)(2,1)} %reshape.90), calls=%async_computation | async-start | bytes 786432 | tf_op jit(solution)/shard_map/all_to_all | solution.py:101
  285.3 123.4 %all-gather.2.cloned.1.call-start = ((), (), s32[]{:S(2)}) async-start(), calls=%async_computation.2 | async-start | bytes 6963200 | tf_op jit(solution)/shard_map/all_gather | solution.py:127
  309.5 8.0 %collective-permute-start = (bf16[2,2048]{1,0:T(2,128)(2,1)S(1)}, bf16[2,2048]{1,0:T(2,128)(2,1)S(1)}, u32[]{:S(2)}, u32[]{:S(2)}) collective-permute-start(bf16[2,2048]{1,0:T(2,128)(2,1)S(1)} %slice.109), channel_id=1, source_target_pairs={{0,16},{16,32},{32,48},{48,64},{64,80},{80,96},{96,112},{112,128},... | collective-permute-start | bytes 24584 | tf_op jit(solution)/shard_map/ppermute | solution.py:23
  312.9 6.8 %copy-start.3 = (bf16[144,32]{0,1:T(8,128)(2,1)S(1)}, bf16[144,32]{0,1:T(8,128)(2,1)}, u32[]{:S(2)}) copy-start(bf16[144,32]{0,1:T(8,128)(2,1)} %param.16) | copy-start | bytes 27652
  312.9 6.8 %copy-start.4 = (f32[32]{0:T(128)S(1)}, f32[32]{0:T(128)}, u32[]{:S(2)}) copy-start(f32[32]{0:T(128)} %param.17) | copy-start | bytes 388
  313.1 5.0 %collective-permute-start.1 = (bf16[2,2048]{1,0:T(2,128)(2,1)S(1)}, bf16[2,2048]{1,0:T(2,128)(2,1)S(1)}, u32[]{:S(2)}, u32[]{:S(2)}) collective-permute-start(bf16[2,2048]{1,0:T(2,128)(2,1)S(1)} %slice.111), channel_id=1, source_target_pairs={{16,0},{32,16},{48,32},{64,48},{80,64},{96,80},{112,96},{128,112},... | collective-permute-start | bytes 24584 | tf_op jit(solution)/shard_map/ppermute | solution.py:24
  408.7 4.7 %copy-start.1 = (bf16[50,512,128]{2,1,0:T(8,128)(2,1)S(1)}, bf16[50,512,128]{2,1,0:T(8,128)(2,1)}, u32[]{:S(2)}) copy-start(bf16[50,512,128]{2,1,0:T(8,128)(2,1)} %all-gather.2.cloned.1.call-done) | copy-start | bytes 19660804
Sparse Core Ops, SparseCore 0:
  78.6 176.9 all-reduce.4
  321.1 87.5 all-gather.1
where the time goes:
time: 450 us; the launch traced here: 444 us
  waiting for transfers between devices  285 us (63%)
  blocking collectives  66.6 us (15%)
  matrix products  32.9 us (7%)
  starting transfers between devices  30.6 us (7%)
  between operations  15 us (3%)
  local copies, waits for them, and re-layouts  9.37 us (2%)
  other arithmetic  5.27 us (1%)
    psum x1, waiting for transfers between devices, shards(): velocity = lax.psum(partial_proj, 'tensor')  176 us
    all_gather x1, waiting for transfers between devices, shards(): gathered = lax.all_gather(activated, 'tensor', axis=1, tiled=True)  86.1 us
    psum x1, blocking collectives, shards(): lax.psum((jnp.sum(feats, axis=-1), jnp.sum(feats * feats, axis=-1)), 'ten...  66.6 us
    dot_general x9, matrix products, conv_three(): jnp.einsum('rkw,ko->row', window, weights[3 * row_off + col_off], preferr...  28.3 us
    all_to_all x1, starting transfers between devices, shards(): lax.all_to_all(sendbuf, 'wide', split_axis=0, concat_axis=0, tiled=True)  25.2 us
    all_to_all x1, waiting for transfers between devices, shards(): lax.all_to_all(sendbuf, 'wide', split_axis=0, concat_axis=0, tiled=True)  21.6 us
  transfers between devices with their start and end apart: 5, of which 4 were waited for; matrix products, arithmetic and copies ran while one was open for 1% of the time, Pallas kernels for 0%

commit v1 on v0

v1 whole, which is shorter than its diff:
```python
import functools

import jax
import jax.numpy as jnp
from jax import lax
from jax.experimental import pallas as pl
from jax.experimental.pallas import tpu as pltpu
from jax.sharding import PartitionSpec as P

D = 3072
LC = 16
GRID = 64
STEPS = 28
WPIX = 128
shift_value = 3.0
norm_eps = 1e-06

F32 = jnp.float32
BF16 = jnp.bfloat16

SR = 24
STAT = 2 * SR
WROW = STAT + 32
BLOCK = WROW + 32


def iota(shape, dim):
    return lax.broadcasted_iota(jnp.int32, shape, dim)


def thirds(value):
    first = value.astype(BF16).astype(F32)
    rest = value - first
    second = rest.astype(BF16).astype(F32)
    return (first, second, (rest - second).astype(BF16).astype(F32))


def to_column(row):
    n = row.shape[1]
    return jnp.sum(jnp.where(iota((n, n), 0) == iota((n, n), 1), row, 0.0), axis=1, keepdims=True)


def to_row(column):
    n = column.shape[0]
    return jnp.sum(jnp.where(iota((n, n), 0) == iota((n, n), 1), column, 0.0), axis=0, keepdims=True)


def project_kernel(rows, peers, here, h_ref, mod_ref, w_ref, win_ref, bin_ref, noisy_ref, send_ref, noisy_out, sums, drawn):
    per = GRID // peers
    feats = h_ref.shape[0]
    weight = w_ref[...].astype(F32)
    scaled = (1.0 + mod_ref[1:2, :]) * weight
    colsum = jnp.sum(scaled, axis=1, keepdims=True)
    shifted = jnp.sum(mod_ref[0:1, :] * weight, axis=1, keepdims=True)
    left = jnp.concatenate(thirds(scaled - colsum / feats), axis=0).astype(BF16)
    lane = iota((1, 128), 1)
    low = lane < 64
    step = 256
    for at in range(0, h_ref.shape[1], step):
        hid = h_ref[:, at : at + step]
        prod = jnp.dot(left, hid, preferred_element_type=F32)
        wide = hid.astype(F32)
        pieces = thirds(jnp.sum(wide, axis=0, keepdims=True)) + thirds(jnp.sum(wide * wide, axis=0, keepdims=True))
        stats = [jnp.broadcast_to(p, (4, step)) for p in pieces] + [jnp.zeros((40, step), F32)]
        both = jnp.concatenate([prod[:64, :] + prod[64:128, :] + prod[128:, :]] + stats, axis=0)
        sums[at : at + step, :] = jnp.transpose(both)
        drawn[at : at + step, :] = jnp.transpose(noisy_ref[:, at : at + step])
    win = win_ref[...].astype(F32)
    outs = win.shape[0]
    rest_w = jnp.concatenate([win[:, 128:], jnp.zeros((outs, 128 - (win.shape[1] - 128)), F32)], axis=1)
    side = pltpu.roll(rest_w, 64, 1)
    for n, piece in enumerate(thirds(to_column(bin_ref[...]))):
        side = jnp.where(lane == 80 + n, piece, side)
    pad = jnp.zeros((1, 64), F32)
    lines = thirds(to_row(colsum)) + thirds(to_row(shifted))
    extra = jnp.concatenate([jnp.concatenate([v, pad], axis=1) for v in lines] + [jnp.zeros((2, 128), F32)], axis=0)
    main_w = win_ref[:, :128]
    fill = [jnp.zeros((SR - rows, 128), F32)] if rows < SR else []
    for peer in range(peers):
        base = peer * BLOCK
        stat = jnp.zeros((SR, 128), F32)
        halves = []
        for dk in range(per):
            val = sums[pl.ds(peer * per + dk, rows, stride=GRID), :]
            val = jnp.concatenate([val] + fill, axis=0) if fill else val
            turned = pltpu.roll(val, 64, 1)
            stat = jnp.where((lane % 4 == dk) & (lane < 24), turned, stat)
            halves.append(val if dk % 2 == 0 else turned)
        for half in range(per // 2):
            joined = jnp.where(low, halves[2 * half], halves[2 * half + 1])
            send_ref[base + half * SR : base + (half + 1) * SR, :] = joined.astype(BF16)
        tile = jnp.concatenate([stat, extra], axis=0) + side
        send_ref[base + STAT : base + STAT + 32, :] = tile.astype(BF16)
        send_ref[base + WROW : base + WROW + 32, :] = main_w
    mine = here[0] * per
    for half in range(per // 2):
        one = drawn[pl.ds(mine + 2 * half, rows, stride=GRID), :]
        two = drawn[pl.ds(mine + 2 * half + 1, rows, stride=GRID), :]
        both = jnp.concatenate([one, two], axis=1)
        noisy_out[half * SR : (half + 1) * SR, :] = jnp.concatenate([both] + fill, axis=0) if fill else both


def spread(tile, at, low):
    parts = []
    for half in range(2):
        a = tile[:, at + 2 * half : at + 2 * half + 1]
        b = tile[:, at + 2 * half + 1 : at + 2 * half + 2]
        parts.append(jnp.where(low, a, b))
    return jnp.concatenate(parts, axis=0)


def clean_kernel(rows, peers, slabs, feats, step_ref, table, recv_ref, noisy_ref, send_ref):
    lane = iota((1, 128), 1)
    low = lane < 64
    total = jnp.zeros((2 * SR, 128), F32)
    means = []
    columns = []
    sums = jnp.zeros((SR, 128), F32)
    shifted = jnp.zeros((1, 128), F32)
    for peer in range(peers):
        base = peer * BLOCK
        total = total + recv_ref[base : base + 2 * SR, :].astype(F32)
        tile = recv_ref[base + STAT : base + STAT + 32, :].astype(F32)
        stat = tile[:SR, :]
        stat = stat + pltpu.roll(stat, 124, 1) + pltpu.roll(stat, 120, 1)
        sums = sums + stat
        means.append(stat / feats)
        cs = jnp.where(low, tile[SR : SR + 1, :] + tile[SR + 1 : SR + 2, :] + tile[SR + 2 : SR + 3, :], 0.0)
        columns.append(cs + pltpu.roll(cs, 64, 1))
        sw = jnp.where(low, tile[SR + 3 : SR + 4, :] + tile[SR + 4 : SR + 5, :] + tile[SR + 5 : SR + 6, :], 0.0)
        shifted = shifted + sw + pltpu.roll(sw, 64, 1)
    mean = sums / (feats * peers)
    for m, cs in zip(means, columns):
        total = total + spread(m - mean, 0, low) * cs
    square = pltpu.roll(mean, 116, 1)
    rstd = 1.0 / jnp.sqrt(square - mean * mean + norm_eps)
    velocity = total * spread(rstd, 0, low) + shifted
    frac = jnp.zeros((1, 128), F32) + step_ref[0].astype(F32)
    frac = frac / STEPS
    sigma = shift_value * frac / (1.0 + (shift_value - 1.0) * frac)
    clean = (noisy_ref[...] - sigma * velocity).astype(BF16).astype(F32)
    held = jnp.concatenate([clean, pltpu.roll(clean, 64, 1), jnp.zeros((128 - 4 * SR, 128), F32)], axis=0).astype(BF16)
    owner = jnp.full((1, 128), -9, jnp.int32)
    for j in range(rows):
        owner = jnp.where((lane % SR == j) & (lane < 4 * SR), table[j], owner)
    shape = (slabs * 8, 128)
    row = iota(shape, 0)
    col = iota(shape, 1)
    slab = row // 8
    upper = row % 8 < 4
    dk = row % 4
    turned = col // (2 * SR)
    half = (col // SR) % 2
    j = col % SR
    right_half = half == dk // 2
    target = jnp.where(upper, owner, jnp.where(j == 0, owner - 1, -9))
    own = target == slab
    take_low = (right_half & (turned == dk % 2) & own).astype(F32).astype(BF16)
    above = upper & (j == rows - 1) & (owner + 1 == slab) & (owner >= 0)
    take_high = (right_half & (turned == 1 - dk % 2) & above).astype(F32).astype(BF16)
    left = jnp.dot(take_low, held, preferred_element_type=F32)
    right = jnp.dot(take_high, held, preferred_element_type=F32)
    send_ref[...] = jnp.where(low, left, right).astype(BF16)


def pick_kernel(rows, peers, slabs, here, table, recv_ref, send_ref, wide):
    wide[...] = recv_ref[...].astype(F32)
    lane = iota((8, 128), 1)
    low = lane < 64
    top = iota((8, 128), 0) < 4
    count = rows + 2
    per = count // 2

    def source(j):
        return lax.rem(2 * here[1] - table[j] + 2 * slabs, slabs)

    def piece(i, at_low, at_top):
        if i == 0:
            x, is_low, is_top = (lax.rem(source(rows - 1) - 1 + slabs, slabs), False, True)
        elif i == count - 1:
            x, is_low, is_top = (lax.rem(source(0) + 1, slabs), True, False)
        else:
            x, is_low, is_top = (source(i - 1), True, True)
        tile = wide[pl.ds(pl.multiple_of(x * 8, 8), 8), :]
        if is_low != at_low:
            tile = pltpu.roll(tile, 64, 1)
        if is_top != at_top:
            tile = pltpu.roll(tile, 4, 0)
        return tile

    for block in range((per + 1) // 2):
        quarters = []
        for at_top in (True, False):
            for at_low in (True, False):
                n = 2 * block + (0 if at_low else 1)
                if n < per:
                    quarters.append(piece(n + (0 if at_top else per), at_low, at_top))
                else:
                    quarters.append(jnp.zeros((8, 128), F32))
        tile = jnp.where(top, jnp.where(low, quarters[0], quarters[1]), jnp.where(low, quarters[2], quarters[3]))
        tile = tile.astype(BF16)
        for peer in range(peers):
            send_ref[peer * 8 : peer * 8 + 8, block * 128 : (block + 1) * 128] = tile


def decode_kernel(
    rows, peers, here, lat_ref, win_ref, w1_ref, b1_ref, dec_ref, res_ref, spread_out, shifted, weight, bias, act, taps
):
    t = here[0]
    slab_height = 2 * rows
    first_row = here[1] * slab_height
    count = rows + 2
    per = count // 2
    outs = w1_ref.shape[0] // 9
    lane = iota((1, 128), 1)
    all_out = peers * outs

    def load_weights(base, at):
        side = pltpu.roll(win_ref[pl.ds(pl.multiple_of(base + STAT, 16), 32), :].astype(F32), 64, 1)
        weight[at : at + outs, :128] = win_ref[pl.ds(pl.multiple_of(base + WROW, 16), 32), :]
        weight[at : at + outs, 128:] = jnp.where(lane < 16, side, 0.0).astype(BF16)
        total = side[:, 16:17] + side[:, 17:18] + side[:, 18:19]
        bias[at : at + outs, :] = jnp.broadcast_to(total, (outs, 128))

    for peer in range(peers):
        load_weights(peer * BLOCK, peer * outs)
    load_weights(t * BLOCK, all_out)

    r = iota((128, 512), 0)
    c = iota((128, 512), 1)
    token = 4 * (r // 8) + r % 4
    hot = ((r // 4) % 2 == c // 256) & (c % 128 == 2 * token + (c // 128) % 2)
    hot = hot.astype(F32).astype(BF16)
    spread_out[...] = lax.dot_general(lat_ref[...], hot, (((0,), (0,)), ((), ())), preferred_element_type=F32)
    for i in range(count):
        for a in range(2):
            at = (i % per) * 64 + a * 32
            base = (i // per) * 256
            pix = spread_out[at : at + 16, base : base + 128] + spread_out[at + 16 : at + 32, base + 128 : base + 256]
            row = (2 * i + a) * 48
            shifted[row : row + 16, :] = jnp.where(lane == 0, 0.0, pltpu.roll(pix, 1, 1)).astype(BF16)
            shifted[row + 16 : row + 32, :] = pix.astype(BF16)
            shifted[row + 32 : row + 48, :] = jnp.where(lane == 127, 0.0, pltpu.roll(pix, 127, 1)).astype(BF16)

    def finish(y):
        global_row = lax.rem(first_row + y, WPIX)
        up = global_row != 0
        down = global_row != WPIX - 1
        sums = taps[y + 1, 96:192, :]
        sums = sums + jnp.where(up, taps[y, 0:96, :], 0.0)
        sums = sums + jnp.where(down, taps[y + 2, 192:288, :], 0.0)
        total = sums[32:64, :] + b1_ref[...]
        total = total + jnp.where(lane == 0, 0.0, pltpu.roll(sums[0:32, :], 1, 1))
        total = total + jnp.where(lane == 127, 0.0, pltpu.roll(sums[64:96, :], 127, 1))
        res_ref[y] = total.astype(BF16)

    def pair(m, carry):
        parts = []
        for n in range(2):
            q = 2 * m + n
            global_row = lax.rem(first_row - 1 + q + WPIX, WPIX)
            block = shifted[pl.ds(pl.multiple_of(q * 48, 16), 144), :]
            up = jnp.where(global_row != 0, block[:48, :], jnp.zeros((48, 128), BF16))
            down = jnp.where(global_row != WPIX - 1, block[96:, :], jnp.zeros((48, 128), BF16))
            parts.append(jnp.concatenate([up, block[48:96, :], down], axis=0))
        right = jnp.concatenate(parts, axis=1)
        feat = jnp.dot(weight[:, :144], right, preferred_element_type=F32)
        both = jnp.concatenate([bias[...], bias[...]], axis=1)
        feat = (feat + both).astype(BF16)

        @pl.when(m > 0)
        def _():
            dec_ref[2 * m - 1] = feat[all_out:, :128]

        @pl.when(m < count - 2)
        def _():
            dec_ref[2 * m] = feat[all_out:, 128:]

        value = feat[:all_out, :].astype(F32)
        halved = 0.5 * value
        act[...] = (halved + halved * jnp.tanh(halved)).astype(BF16)
        tap = jnp.dot(w1_ref[...], act[...], preferred_element_type=F32)
        taps[2 * m] = tap[:, :128]
        taps[2 * m + 1] = tap[:, 128:]

        @pl.when(m > 0)
        def _():
            finish(2 * m - 2)
            finish(2 * m - 1)

        return carry

    lax.fori_loop(0, rows + 1, pair, 0)


def vmem():
    return pl.BlockSpec(memory_space=pltpu.VMEM)


def smem():
    return pl.BlockSpec(memory_space=pltpu.SMEM)


def call(body, inputs, kinds, out_shape, scratch, flops, bytes_accessed, limit):
    return pl.pallas_call(
        body,
        out_shape=out_shape,
        in_specs=[smem() if k == "s" else vmem() for k in kinds],
        out_specs=jax.tree.map(lambda _: vmem(), out_shape),
        scratch_shapes=scratch,
        compiler_params=pltpu.CompilerParams(vmem_limit_bytes=limit << 20),
        cost_estimate=pl.CostEstimate(flops=flops, bytes_accessed=bytes_accessed, transcendentals=0),
    )(*inputs)


def shards(
    hidden,
    modulation,
    final_weight,
    noisy,
    step_index,
    slab_table,
    conv_in_weight,
    conv_in_bias,
    conv1_weight,
    conv1_bias,
):
    peers = lax.axis_size("tensor")
    slabs = lax.axis_size("wide")
    t = lax.axis_index("tensor")
    w = lax.axis_index("wide")
    here = jnp.stack([t, w]).astype(jnp.int32)
    rows = slab_table.shape[0]
    feats = hidden.shape[1]
    outs = conv_in_weight.shape[1]
    sds = jax.ShapeDtypeStruct

    send, noisy_mine = call(
        functools.partial(project_kernel, rows, peers),
        (here, hidden.T, modulation, final_weight.T, conv_in_weight.T, conv_in_bias.reshape(1, -1), noisy.T),
        "svvvvvv",
        (sds((peers * BLOCK, 128), BF16), sds((2 * SR, 128), F32)),
        [pltpu.VMEM((rows * GRID, 128), F32), pltpu.VMEM((rows * GRID, 64), F32)],
        10**9,
        2 * 10**6,
        16,
    )
    recv = lax.all_to_all(send, "tensor", split_axis=0, concat_axis=0, tiled=True)
    routed = call(
        functools.partial(clean_kernel, rows, peers, slabs, feats),
        (step_index, slab_table, recv, noisy_mine),
        "ssvv",
        sds((slabs * 8, 128), BF16),
        [],
        10**7,
        10**6,
        8,
    )
    landed = lax.all_to_all(routed, "wide", split_axis=0, concat_axis=0, tiled=True)
    width = 128 * (((rows + 2) // 2 + 1) // 2)
    copies = call(
        functools.partial(pick_kernel, rows, peers, slabs),
        (here, slab_table, landed),
        "ssv",
        sds((peers * 8, width), BF16),
        [pltpu.VMEM((slabs * 8, 128), F32)],
        10**6,
        10**6,
        8,
    )
    latents = lax.all_to_all(copies, "tensor", split_axis=0, concat_axis=0, tiled=True)
    own = lax.dynamic_slice_in_dim(conv1_weight, t * outs, outs, 2)
    w1 = own.transpose(0, 2, 1).reshape(9 * outs, -1)
    b1 = jnp.broadcast_to(lax.dynamic_slice_in_dim(conv1_bias, t * outs, outs, 0)[:, None], (outs, 128))
    channels = w1.shape[1]
    return call(
        functools.partial(decode_kernel, rows, peers),
        (here, latents, recv, w1, b1),
        "svvvv",
        (sds((2 * rows, outs, WPIX), BF16), sds((2 * rows, outs, WPIX), BF16)),
        [
            pltpu.VMEM((width // 128 * 128, 512), F32),
            pltpu.VMEM((2 * (rows + 2) * 48, 128), BF16),
            pltpu.VMEM((channels + outs, 256), BF16),
            pltpu.VMEM((channels + outs, 128), F32),
            pltpu.VMEM((channels, 256), BF16),
            pltpu.VMEM((2 * rows + 2, 9 * outs, 128), F32),
        ],
        6 * 10**9,
        3 * 10**6,
        24,
    )


def solution(mesh):
    return jax.shard_map(
        shards,
        mesh=mesh,
        in_specs=(
            P("wide", "tensor"),
            P(None, "tensor"),
            P("tensor", None),
            P("wide", None),
            P(),
            P("wide"),
            P(None, "tensor"),
            P("tensor"),
            P(),
            P(),
        ),
        out_specs=(P("wide", "tensor", None), P("wide", "tensor", None)),
        check_vma=False,
    )
```

time: 450 us -> 102 us (0.23); the launches traced: 444 us -> 102 us
  waiting for transfers between devices: 285 us -> 16.5 us
  matrix products: 32.9 us -> 0 us
  blocking collectives: 66.6 us -> 38.5 us
  Pallas kernels: 0 us -> 25.1 us
  starting transfers between devices: 30.6 us -> 11.9 us
  between operations: 15 us -> 1.33 us
  other arithmetic: 5.27 us -> 0.08 us
    psum x1 -> x0, waiting for transfers between devices: 176 us -> none  [shards(): velocity = lax.psum(partial_proj, 'tensor')]
    all_gather x1 -> x0, waiting for transfers between devices: 86.1 us -> none  [shards(): gathered = lax.all_gather(activated, 'tensor', axis=1, tiled=True)]
    psum x1 -> x0, blocking collectives: 66.6 us -> none  [shards(): lax.psum((jnp.sum(feats, axis=-1), jnp.sum(feats * feats, axis=-1)), 'ten...]
    all_to_all x0 -> x1, blocking collectives: none -> 38.5 us  [shards(): lax.all_to_all(routed, 'wide', split_axis=0, concat_axis=0, tiled=True)]
    dot_general x13 -> x0, matrix products: 32.9 us -> none  [the longest x9 28.3 us: conv_three(): jnp.einsum('rkw,ko->row', window, weights[3 * row_off + col_off], preferr...]
    pallas_call x0 -> x4, Pallas kernels: none -> 25.1 us  [call(): pl.pallas_call(body, out_shape=out_shape, in_specs=[smem() if k == 's' el...]
    all_to_all x1 -> x2, starting transfers between devices: 25.2 us -> 11.9 us  [the longest x1 7.99 us: shards(): lax.all_to_all(send, 'tensor', split_axis=0, concat_axis=0, tiled=True)]
    ppermute x2 -> x0, starting transfers between devices: 5.33 us -> none  [the longest x1 3.41 us: padded_2(): before = lax.ppermute(last, axis, up)]
  transfers between devices with their start and end apart: 5 -> 2, of which waited for: 4 -> 2; matrix products, arithmetic and copies ran while one was open for 1% -> 3% of each run, Pallas kernels for 0% -> 0%
where the time goes in v1:
time: 102 us
  blocking collectives  38.5 us (38%)
  Pallas kernels  25.1 us (25%)
  waiting for transfers between devices  16.5 us (16%)
  starting transfers between devices  11.9 us (12%)
  local copies, waits for them, and re-layouts  8.42 us (8%)
  between operations  1.33 us (1%)
    all_to_all x1, blocking collectives, shards(): lax.all_to_all(routed, 'wide', split_axis=0, concat_axis=0, tiled=True)  38.5 us
    pallas_call x4, Pallas kernels, call(): pl.pallas_call(body, out_shape=out_shape, in_specs=[smem() if k == 's' el...  25.1 us
    all_to_all x1, waiting for transfers between devices, shards(): lax.all_to_all(send, 'tensor', split_axis=0, concat_axis=0, tiled=True)  10 us
    all_to_all x1, starting transfers between devices, shards(): lax.all_to_all(send, 'tensor', split_axis=0, concat_axis=0, tiled=True)  7.99 us
    all_to_all x1, waiting for transfers between devices, shards(): lax.all_to_all(copies, 'tensor', split_axis=0, concat_axis=0, tiled=True)  6.49 us
    unnamed x16, local copies, waits for them, and re-layouts  5.53 us
    all_to_all x1, starting transfers between devices, shards(): lax.all_to_all(copies, 'tensor', split_axis=0, concat_axis=0, tiled=True)  3.93 us
    transpose x2, local copies, waits for them, and re-layouts, shards(): w1 = own.transpose(0, 2, 1).reshape(9 * outs, -1)  2.05 us
  transfers between devices with their start and end apart: 2, of which 2 were waited for; matrix products, arithmetic and copies ran while one was open for 3% of the time, Pallas kernels for 0%

profile of v1, /device:TPU:1, one launch (start us, length us, event | category | flops | bytes accessed | tf_op | source)
XLA Modules:
  0.0 101.8 jit_solution(3087565151360970982)
XLA Ops:
  0.6 0.0 copy-start.1
  0.7 0.1 pad_add_fusion.here
  0.7 0.0 copy-start.2
  0.7 1.1 %copy-done.2 = bf16[1536,192]{0,1:T(8,128)(2,1)S(1)} copy-done((bf16[1536,192]{0,1:T(8,128)(2,1)S(1)}, bf16[1536,192]{0,1:T(8,128)(2,1)}, u32[]{:S(2)}) %copy-start.2) | copy-done | bytes 589848
  1.8 0.0 copy-start.3
  1.8 1.0 copy-done.3
  2.8 0.0 copy-start.4
  2.8 0.8 copy-done.4
  3.5 0.0 copy-start.5
  3.5 0.7 copy-done.5
  4.3 0.0 copy-start.6
  4.3 0.7 copy-done.6
  4.9 0.0 copy-start.7
  4.9 0.7 copy-done.7
  5.6 2.4 %shard_map.113 = (bf16[1792,128]{1,0:T(8,128)(2,1)}, f32[48,128]{1,0:T(8,128)S(1)}) custom-call(s32[2]{0:T(128)S(1)} %pad_add_fusion.here, bf16[192,1536]{1,0:T(8,128)(2,1)S(1)} %bitcast.22, f32[2,192]{1,0:T(2,128)S(1)} %copy-done.6, bf16[64,192]{1,0:T(8,128)(2,1)S(1)} %bitcast.24, bf16[32,144]{1,0:T(8,128)(2,1)S(1)} %bitcast.25, f32[1,32]{1,0:T(1,128)S(1)} %bitcast.26, ...), custom_call_target="tpu_custom_call" | custom-call | flops 1000000000 | bytes 2000000 | tf_op jit(solution)/shard_map/pallas_call | solution.py:305
  8.0 8.0 %all-to-all-start = ((bf16[16,112,128]{2,1,0:T(8,128)(2,1)}), bf16[16,112,128]{2,1,0:T(8,128)(2,1)S(1)}, u32[]{:S(2)}, u32[]{:S(2)}) async-start(bf16[16,112,128]{2,1,0:T(8,128)(2,1)} %bitcast.7), calls=%async_computation | async-start | bytes 917504 | tf_op jit(solution)/shard_map/all_to_all | solution.py:348
  16.6 10.0 %all-to-all-done = bf16[16,112,128]{2,1,0:T(8,128)(2,1)S(1)} async-done(((bf16[16,112,128]{2,1,0:T(8,128)(2,1)}), bf16[16,112,128]{2,1,0:T(8,128)(2,1)S(1)}, u32[]{:S(2)}, u32[]{:S(2)}) %all-to-all-start) | async-done | bytes 458784 | tf_op jit(solution)/shard_map/all_to_all | solution.py:348
  26.7 0.0 copy-start
  26.7 0.7 copy-done
  27.3 1.4 %shard_map.114 = bf16[384,128]{1,0:T(8,128)(2,1)S(1)} custom-call(s32[1]{0:T(128)S(6)} %copy.13.step_ref, s32[24]{0:T(128)S(1)} %copy-done, bf16[1792,128]{1,0:T(8,128)(2,1)S(1)} %bitcast.16, f32[48,128]{1,0:T(8,128)S(1)} %get-tuple-element.5.noisy_ref), custom_call_target="tpu_custom_call" | custom-call | flops 10000000 | bytes 1000000 | tf_op jit(solution)/shard_map/pallas_call | solution.py:305
  28.7 38.5 %all_to_all.33 = bf16[48,8,128]{2,1,0:T(8,128)(2,1)S(1)} all-to-all(bf16[48,8,128]{2,1,0:T(8,128)(2,1)S(1)} %bitcast.18), channel_id=1, replica_groups=mesh['wide'=48,'tensor'=16] {'wide'}, dimensions={0} | all-to-all | bytes 196608 | tf_op jit(solution)/shard_map/all_to_all | solution.py:359
  67.2 0.0 copy-done.1
  67.2 1.4 %shard_map.115 = bf16[128,896]{1,0:T(8,128)(2,1)} custom-call(s32[2]{0:T(128)S(1)} %pad_add_fusion.here, s32[24]{0:T(128)S(1)} %copy-done.1, bf16[384,128]{1,0:T(8,128)(2,1)S(1)} %bitcast.19), custom_call_target="tpu_custom_call" | custom-call | flops 1000000 | bytes 1000000 | tf_op jit(solution)/shard_map/pallas_call | solution.py:305
  68.6 3.9 %all-to-all-start.2 = ((bf16[16,8,896]{2,1,0:T(8,128)(2,1)}), bf16[16,8,896]{2,1,0:T(8,128)(2,1)S(1)}, u32[]{:S(2)}, u32[]{:S(2)}) async-start(bf16[16,8,896]{2,1,0:T(8,128)(2,1)} %bitcast.11), calls=%async_computation.2 | async-start | bytes 458752 | tf_op jit(solution)/shard_map/all_to_all | solution.py:371
  72.5 1.7 %dynamic-slice_bitcast_fusion = bf16[9,32,512]{1,2,0:T(8,128)(2,1)S(1)} fusion(bf16[9,512,512]{2,1,0:T(8,128)(2,1)} %param.18, s32[]{:T(128)S(6)} %select_n.4), kind=kLoop, calls=%fused_computation | loop fusion | bytes 589828 | tf_op jit(solution)/shard_map/transpose | solution.py:373
  74.2 0.4 copy.12
  74.6 0.8 dynamic_slice.7
  75.4 6.5 %all-to-all-done.2 = bf16[16,8,896]{2,1,0:T(8,128)(2,1)S(1)} async-done(((bf16[16,8,896]{2,1,0:T(8,128)(2,1)}), bf16[16,8,896]{2,1,0:T(8,128)(2,1)S(1)}, u32[]{:S(2)}, u32[]{:S(2)}) %all-to-all-start.2) | async-done | bytes 229408 | tf_op jit(solution)/shard_map/all_to_all | solution.py:371
  81.8 0.1 broadcast_in_dim.2.b1_ref
  81.9 19.9 %shard_map.116 = (bf16[48,32,128]{2,1,0:T(8,128)(2,1)}, bf16[48,32,128]{2,1,0:T(8,128)(2,1)}) custom-call(s32[2]{0:T(128)S(1)} %pad_add_fusion.here, bf16[128,896]{1,0:T(8,128)(2,1)S(1)} %bitcast.21, bf16[1792,128]{1,0:T(8,128)(2,1)S(1)} %bitcast.17, bf16[288,512]{1,0:T(8,128)(2,1)S(1)} %bitcast.20, f32[32,128]{1,0:T(8,128)S(1)} %broadcast_in_dim.2.b1_ref), custom_call_target="tpu_custom_call" | custom-call | flops 6000000000 | bytes 3000000 | tf_op jit(solution)/shard_map/pallas_call | solution.py:305
Async XLA Ops:
  0.6 66.6 %copy-start.1 = (s32[24]{0:T(128)S(1)}, s32[24]{0:T(128)}, u32[]{:S(2)}) copy-start(s32[24]{0:T(128)} %table.3) | copy-start | bytes 292
  0.7 1.1 %copy-start.2 = (bf16[1536,192]{0,1:T(8,128)(2,1)S(1)}, bf16[1536,192]{0,1:T(8,128)(2,1)}, u32[]{:S(2)}) copy-start(bf16[1536,192]{0,1:T(8,128)(2,1)} %param.10) | copy-start | bytes 1769476
  1.8 1.0 copy-start.3
  2.8 0.8 copy-start.4
  3.5 0.7 copy-start.5
  4.3 0.7 copy-start.6
  4.9 0.7 copy-start.7
  8.0 18.7 %all-to-all-start = ((bf16[16,112,128]{2,1,0:T(8,128)(2,1)}), bf16[16,112,128]{2,1,0:T(8,128)(2,1)S(1)}, u32[]{:S(2)}, u32[]{:S(2)}) async-start(bf16[16,112,128]{2,1,0:T(8,128)(2,1)} %bitcast.7), calls=%async_computation | async-start | bytes 917504 | tf_op jit(solution)/shard_map/all_to_all | solution.py:348
  26.7 0.7 copy-start
  68.6 13.2 %all-to-all-start.2 = ((bf16[16,8,896]{2,1,0:T(8,128)(2,1)}), bf16[16,8,896]{2,1,0:T(8,128)(2,1)S(1)}, u32[]{:S(2)}, u32[]{:S(2)}) async-start(bf16[16,8,896]{2,1,0:T(8,128)(2,1)} %bitcast.11), calls=%async_computation.2 | async-start | bytes 458752 | tf_op jit(solution)/shard_map/all_to_all | solution.py:371

commit v2 on v1

v2 whole, which is shorter than its diff:
```python
import functools

import jax
import jax.numpy as jnp
from jax import lax
from jax.experimental import pallas as pl
from jax.experimental.pallas import tpu as pltpu
from jax.sharding import PartitionSpec as P

D = 3072
LC = 16
GRID = 64
STEPS = 28
WPIX = 128
shift_value = 3.0
norm_eps = 1e-06

F32 = jnp.float32
BF16 = jnp.bfloat16

SR = 24
STAT = 2 * SR
WROW = STAT + 16
BLOCK = WROW + 32


def iota(shape, dim):
    return lax.broadcasted_iota(jnp.int32, shape, dim)


def thirds(value):
    first = value.astype(BF16).astype(F32)
    rest = value - first
    second = rest.astype(BF16).astype(F32)
    return (first, second, (rest - second).astype(BF16).astype(F32))


def to_column(row):
    n = row.shape[1]
    return jnp.sum(jnp.where(iota((n, n), 0) == iota((n, n), 1), row, 0.0), axis=1, keepdims=True)


def to_row(column):
    n = column.shape[0]
    return jnp.sum(jnp.where(iota((n, n), 0) == iota((n, n), 1), column, 0.0), axis=0, keepdims=True)


def project_kernel(rows, peers, here, h_hbm, noisy_hbm, *rest):
    small = rest[:4]
    send_ref, side_ref, h_ref, noisy_ref, mod_ref, w_ref, win_ref, bin_ref, sums, drawn, sems = rest[4:]
    moves = zip((h_hbm, *small, noisy_hbm), (h_ref, mod_ref, w_ref, win_ref, bin_ref, noisy_ref))
    copies = [pltpu.make_async_copy(src, dst, sems.at[n]) for n, (src, dst) in enumerate(moves)]
    for copy in copies:
        copy.start()
    for copy in copies[1:5]:
        copy.wait()
    per = GRID // peers
    feats = h_ref.shape[0]
    weight = w_ref[...].astype(F32)
    scaled = (1.0 + mod_ref[1:2, :]) * weight
    colsum = jnp.sum(scaled, axis=1, keepdims=True)
    shifted = jnp.sum(mod_ref[0:1, :] * weight, axis=1, keepdims=True)
    left = jnp.concatenate(thirds(scaled - colsum / feats), axis=0).astype(BF16)
    lane = iota((1, 128), 1)
    low = lane < 64
    step = 256
    copies[0].wait()
    for at in range(0, h_ref.shape[1], step):
        hid = h_ref[:, at : at + step]
        prod = jnp.dot(left, hid, preferred_element_type=F32)
        wide = hid.astype(F32)
        pieces = thirds(jnp.sum(wide, axis=0, keepdims=True)) + thirds(jnp.sum(wide * wide, axis=0, keepdims=True))
        stats = [jnp.broadcast_to(p, (4, step)) for p in pieces] + [jnp.zeros((40, step), F32)]
        both = jnp.concatenate([prod[:64, :] + prod[64:128, :] + prod[128:, :]] + stats, axis=0)
        sums[at : at + step, :] = jnp.transpose(both)
    win = win_ref[...].astype(F32)
    outs = win.shape[0]
    rest_w = jnp.concatenate([win[:, 128:], jnp.zeros((outs, 128 - (win.shape[1] - 128)), F32)], axis=1)
    bias = jnp.zeros((outs, 128), F32)
    for n, piece in enumerate(thirds(to_column(bin_ref[...]))):
        bias = jnp.where(lane == n, piece, bias)
    pad = jnp.zeros((1, 64), F32)
    lines = thirds(to_row(colsum)) + thirds(to_row(shifted))
    lower = jnp.concatenate([jnp.concatenate([v, pad], axis=1) for v in lines] + [jnp.zeros((2, 128), F32)], axis=0)
    upper = jnp.zeros((8, 128), F32)
    for g in range(outs // 8):
        upper = upper + pltpu.roll(bias[8 * g : 8 * g + 8, :], 72 + 4 * g, 1)
        lower = lower + pltpu.roll(rest_w[8 * g : 8 * g + 8, :], 64 + 16 * g, 1)
    main_w = win_ref[:, :128]
    fill = [jnp.zeros((SR - rows, 128), F32)] if rows < SR else []
    for peer in range(peers):
        base = peer * BLOCK
        stat = jnp.zeros((SR, 128), F32)
        halves = []
        for dk in range(per):
            val = sums[pl.ds(peer * per + dk, rows, stride=GRID), :]
            val = jnp.concatenate([val] + fill, axis=0) if fill else val
            turned = pltpu.roll(val, 64, 1)
            stat = jnp.where((lane % 4 == dk) & (lane < 24), turned, stat)
            halves.append(val if dk % 2 == 0 else turned)
        for half in range(per // 2):
            joined = jnp.where(low, halves[2 * half], halves[2 * half + 1])
            send_ref[base + half * SR : base + (half + 1) * SR, :] = joined.astype(BF16)
        tile = upper
        for g in range(SR // 8):
            tile = tile + (pltpu.roll(stat[8 * g : 8 * g + 8, :], 24 * g, 1) if g else stat[:8, :])
        send_ref[base + STAT : base + STAT + 16, :] = jnp.concatenate([tile, lower], axis=0).astype(BF16)
        send_ref[base + WROW : base + WROW + 32, :] = main_w
    owner = jnp.full((8, 128), -9, jnp.int32)
    for j in range(rows):
        owner = jnp.where((lane % SR == j) & (lane < 4 * SR), here[3 + j], owner)
    frac = (jnp.zeros((8, 128), F32) + here[2].astype(F32)) / STEPS
    sigma = shift_value * frac / (1.0 + (shift_value - 1.0) * frac)
    side_ref[2 * SR : 2 * SR + 8, :] = owner.astype(F32)
    side_ref[2 * SR + 8 : 2 * SR + 16, :] = sigma
    copies[5].wait()
    for at in range(0, h_ref.shape[1], step):
        drawn[at : at + step, :] = jnp.transpose(noisy_ref[:, at : at + step])
    mine = here[0] * per
    for half in range(per // 2):
        one = drawn[pl.ds(mine + 2 * half, rows, stride=GRID), :]
        two = drawn[pl.ds(mine + 2 * half + 1, rows, stride=GRID), :]
        both = jnp.concatenate([one, two], axis=1)
        side_ref[half * SR : (half + 1) * SR, :] = jnp.concatenate([both] + fill, axis=0) if fill else both


def spread(tile, at, low):
    parts = []
    for half in range(2):
        a = tile[:, at + 2 * half : at + 2 * half + 1]
        b = tile[:, at + 2 * half + 1 : at + 2 * half + 2]
        parts.append(jnp.where(low, a, b))
    return jnp.concatenate(parts, axis=0)


def clean_kernel(rows, peers, slabs, feats, recv_ref, side_ref, send_ref):
    lane = iota((1, 128), 1)
    low = lane < 64
    total = jnp.zeros((2 * SR, 128), F32)
    means = []
    columns = []
    sums = jnp.zeros((SR, 128), F32)
    shifted = jnp.zeros((1, 128), F32)
    for peer in range(peers):
        base = peer * BLOCK
        total = total + recv_ref[base : base + 2 * SR, :].astype(F32)
        tile = recv_ref[base + STAT : base + STAT + 16, :].astype(F32)
        upper = tile[:8, :]
        lines = tile[8:, :]
        stat = jnp.concatenate([upper, pltpu.roll(upper, 104, 1), pltpu.roll(upper, 80, 1)], axis=0)
        stat = stat + pltpu.roll(stat, 124, 1) + pltpu.roll(stat, 120, 1)
        sums = sums + stat
        means.append(stat / feats)
        cs = jnp.where(low, lines[0:1, :] + lines[1:2, :] + lines[2:3, :], 0.0)
        columns.append(cs + pltpu.roll(cs, 64, 1))
        sw = jnp.where(low, lines[3:4, :] + lines[4:5, :] + lines[5:6, :], 0.0)
        shifted = shifted + sw + pltpu.roll(sw, 64, 1)
    mean = sums / (feats * peers)
    for m, cs in zip(means, columns):
        total = total + spread(m - mean, 0, low) * cs
    square = pltpu.roll(mean, 116, 1)
    rstd = 1.0 / jnp.sqrt(square - mean * mean + norm_eps)
    velocity = total * spread(rstd, 0, low) + shifted
    sigma = side_ref[2 * SR + 8 : 2 * SR + 9, :]
    clean = (side_ref[: 2 * SR, :] - sigma * velocity).astype(BF16).astype(F32)
    held = jnp.concatenate([clean, pltpu.roll(clean, 64, 1), jnp.zeros((128 - 4 * SR, 128), F32)], axis=0).astype(BF16)
    owner = side_ref[2 * SR : 2 * SR + 1, :].astype(jnp.int32)
    shape = (slabs * 8, 128)
    row = iota(shape, 0)
    col = iota(shape, 1)
    slab = row // 8
    upper = row % 8 < 4
    dk = row % 4
    turned = col // (2 * SR)
    half = (col // SR) % 2
    j = col % SR
    right_half = half == dk // 2
    target = jnp.where(upper, owner, jnp.where(j == 0, owner - 1, -9))
    own = target == slab
    take_low = (right_half & (turned == dk % 2) & own).astype(F32).astype(BF16)
    above = upper & (j == rows - 1) & (owner + 1 == slab) & (owner >= 0)
    take_high = (right_half & (turned == 1 - dk % 2) & above).astype(F32).astype(BF16)
    left = jnp.dot(take_low, held, preferred_element_type=F32)
    right = jnp.dot(take_high, held, preferred_element_type=F32)
    send_ref[...] = jnp.where(low, left, right).astype(BF16)


def pick_kernel(rows, peers, slabs, here, recv_ref, send_ref, wide):
    wide[...] = recv_ref[...].astype(F32)
    lane = iota((8, 128), 1)
    low = lane < 64
    top = iota((8, 128), 0) < 4
    count = rows + 2
    per = count // 2

    def source(j):
        return lax.rem(2 * here[1] - here[3 + j] + 2 * slabs, slabs)

    def piece(i, at_low, at_top):
        if i == 0:
            x, is_low, is_top = (lax.rem(source(rows - 1) - 1 + slabs, slabs), False, True)
        elif i == count - 1:
            x, is_low, is_top = (lax.rem(source(0) + 1, slabs), True, False)
        else:
            x, is_low, is_top = (source(i - 1), True, True)
        tile = wide[pl.ds(pl.multiple_of(x * 8, 8), 8), :]
        if is_low != at_low:
            tile = pltpu.roll(tile, 64, 1)
        if is_top != at_top:
            tile = pltpu.roll(tile, 4, 0)
        return tile

    for block in range((per + 1) // 2):
        quarters = []
        for at_top in (True, False):
            for at_low in (True, False):
                n = 2 * block + (0 if at_low else 1)
                if n < per:
                    quarters.append(piece(n + (0 if at_top else per), at_low, at_top))
                else:
                    quarters.append(jnp.zeros((8, 128), F32))
        tile = jnp.where(top, jnp.where(low, quarters[0], quarters[1]), jnp.where(low, quarters[2], quarters[3]))
        tile = tile.astype(BF16)
        for peer in range(peers):
            send_ref[peer * 8 : peer * 8 + 8, block * 128 : (block + 1) * 128] = tile


def gather_kernel(peers, here, recv_ref, weight, bias):
    lane = iota((1, 128), 1)
    outs = weight.shape[0] // (peers + 1)

    def load(base, at):
        tile = recv_ref[pl.ds(pl.multiple_of(base + STAT, 16), 16), :].astype(F32)
        groups = range(outs // 8)
        side = jnp.concatenate([pltpu.roll(tile[8:, :], 64 - 16 * g, 1) for g in groups], axis=0)
        turned = jnp.concatenate([pltpu.roll(tile[:8, :], 56 - 4 * g, 1) for g in groups], axis=0)
        weight[at : at + outs, :128] = recv_ref[pl.ds(pl.multiple_of(base + WROW, 16), 32), :]
        weight[at : at + outs, 128:] = side[:, :16].astype(BF16)
        total = turned[:, 0:1] + turned[:, 1:2] + turned[:, 2:3]
        bias[at : at + outs, :] = jnp.broadcast_to(total, (outs, 128))

    for peer in range(peers):
        load(peer * BLOCK, peer * outs)
    load(here[0] * BLOCK, peers * outs)


def decode_kernel(rows, here, lat_ref, weight, bias, w1_ref, b1_ref, dec_ref, res_ref, spread_out, shifted, act, act2, taps):
    slab_height = 2 * rows
    first_row = here[1] * slab_height
    count = rows + 2
    per = count // 2
    outs = w1_ref.shape[0] // 9
    lane = iota((1, 128), 1)
    all_out = w1_ref.shape[1]

    r = iota((128, 512), 0)
    c = iota((128, 512), 1)
    token = 4 * (r // 8) + r % 4
    hot = ((r // 4) % 2 == c // 256) & (c % 128 == 2 * token + (c // 128) % 2)
    hot = hot.astype(F32).astype(BF16)
    spread_out[...] = lax.dot_general(lat_ref[...], hot, (((0,), (0,)), ((), ())), preferred_element_type=F32)
    for i in range(count):
        for a in range(2):
            at = (i % per) * 64 + a * 32
            base = (i // per) * 256
            pix = spread_out[at : at + 16, base : base + 128] + spread_out[at + 16 : at + 32, base + 128 : base + 256]
            row = (2 * i + a) * 48
            shifted[row : row + 16, :] = jnp.where(lane == 0, 0.0, pltpu.roll(pix, 1, 1)).astype(BF16)
            shifted[row + 16 : row + 32, :] = pix.astype(BF16)
            shifted[row + 32 : row + 48, :] = jnp.where(lane == 127, 0.0, pltpu.roll(pix, 127, 1)).astype(BF16)

    def features(m, buf):
        parts = []
        for n in range(2):
            q = 2 * m + n
            global_row = lax.rem(first_row - 1 + q + WPIX, WPIX)
            block = shifted[pl.ds(pl.multiple_of(q * 48, 16), 144), :]
            up = jnp.where(global_row != 0, block[:48, :], jnp.zeros((48, 128), BF16))
            down = jnp.where(global_row != WPIX - 1, block[96:, :], jnp.zeros((48, 128), BF16))
            parts.append(jnp.concatenate([up, block[48:96, :], down], axis=0))
        right = jnp.concatenate(parts, axis=1)
        feat = jnp.dot(weight[...], right, preferred_element_type=F32)
        both = jnp.concatenate([bias[...], bias[...]], axis=1)
        feat = (feat + both).astype(BF16)
        dec_ref[jnp.minimum(2 * m, slab_height - 1)] = feat[all_out:, 128:]
        dec_ref[jnp.abs(2 * m - 1)] = feat[all_out:, :128]
        value = feat[:all_out, :].astype(F32)
        halved = 0.5 * value
        buf[...] = (halved + halved * jnp.tanh(halved)).astype(BF16)

    def multiply(m, buf):
        tap = jnp.dot(w1_ref[...], buf[...], preferred_element_type=F32)
        taps[2 * m] = tap[:, :128]
        taps[2 * m + 1] = tap[:, 128:]

    def finish(m):
        for y in (2 * m - 2, 2 * m - 1):
            global_row = lax.rem(first_row + y, WPIX)
            sums = taps[y + 1, 3 * outs : 6 * outs, :]
            sums = sums + jnp.where(global_row != 0, taps[y, 0 : 3 * outs, :], 0.0)
            sums = sums + jnp.where(global_row != WPIX - 1, taps[y + 2, 6 * outs :, :], 0.0)
            total = sums[outs : 2 * outs, :] + b1_ref[...]
            total = total + jnp.where(lane == 0, 0.0, pltpu.roll(sums[0:outs, :], 1, 1))
            total = total + jnp.where(lane == 127, 0.0, pltpu.roll(sums[2 * outs :, :], 127, 1))
            res_ref[y] = total.astype(BF16)

    features(0, act)
    taps[0:4] = jnp.zeros((4, 9 * outs, 128), F32)

    def double(step, carry):
        for n, (now, before) in enumerate(((act2, act), (act, act2))):
            m = 2 * step + 1 + n
            features(m, now)
            multiply(m - 1, before)
            finish(jnp.maximum(m - 2, 1))
        return carry

    lax.fori_loop(0, rows // 2, double, 0)
    multiply(rows, act)
    finish(rows - 1)
    finish(rows)


SPACES = {"s": pltpu.SMEM, "v": pltpu.VMEM, "h": pltpu.HBM}


def call(body, inputs, kinds, out_shape, scratch, flops, bytes_accessed, limit):
    return pl.pallas_call(
        body,
        out_shape=out_shape,
        in_specs=[pl.BlockSpec(memory_space=SPACES[k]) for k in kinds],
        out_specs=jax.tree.map(lambda _: pl.BlockSpec(memory_space=pltpu.VMEM), out_shape),
        scratch_shapes=scratch,
        compiler_params=pltpu.CompilerParams(vmem_limit_bytes=limit << 20),
        cost_estimate=pl.CostEstimate(flops=flops, bytes_accessed=bytes_accessed, transcendentals=0),
    )(*inputs)


def decode_call(rows, here, latents, weight, bias, w1, b1):
    width = latents.shape[1]
    outs = w1.shape[0] // 9
    channels = w1.shape[1]
    shape = jax.ShapeDtypeStruct((2 * rows, outs, WPIX), BF16)
    return call(
        functools.partial(decode_kernel, rows),
        (here, latents, weight, bias, w1, b1),
        "svvvvv",
        (shape, shape),
        [
            pltpu.VMEM((width, 512), F32),
            pltpu.VMEM((2 * (rows + 2) * 48, 128), BF16),
            pltpu.VMEM((channels, 256), BF16),
            pltpu.VMEM((channels, 256), BF16),
            pltpu.VMEM((2 * rows + 2, 9 * outs, 128), F32),
        ],
        6 * 10**9,
        3 * 10**6,
        24,
    )


def gather_call(here, recv, peers, outs):
    sds = jax.ShapeDtypeStruct
    many = (peers + 1) * outs
    return call(
        functools.partial(gather_kernel, peers),
        (here, recv),
        "sv",
        (sds((many, 144), BF16), sds((many, 128), F32)),
        [],
        10**6,
        10**6,
        8,
    )


def shards(
    hidden,
    modulation,
    final_weight,
    noisy,
    step_index,
    slab_table,
    conv_in_weight,
    conv_in_bias,
    conv1_weight,
    conv1_bias,
):
    peers = lax.axis_size("tensor")
    slabs = lax.axis_size("wide")
    t = lax.axis_index("tensor")
    w = lax.axis_index("wide")
    here = jnp.concatenate([jnp.stack([t, w]).astype(jnp.int32), step_index, slab_table])
    rows = slab_table.shape[0]
    tokens, feats = hidden.shape
    outs = conv_in_weight.shape[1]
    sds = jax.ShapeDtypeStruct
    large = (hidden.T, noisy.T)
    small = (modulation, final_weight.T, conv_in_weight.T, conv_in_bias.reshape(1, -1))

    send, side = call(
        functools.partial(project_kernel, rows, peers),
        (here, hidden.T, noisy.T, *small),
        "shhhhhh",
        (sds((peers * BLOCK, 128), BF16), sds((2 * SR + 16, 128), F32)),
        [pltpu.VMEM(x.shape, x.dtype) for x in large + small]
        + [pltpu.VMEM((tokens, 128), F32), pltpu.VMEM((tokens, noisy.shape[1]), F32), pltpu.SemaphoreType.DMA((6,))],
        10**9,
        2 * 10**6,
        60,
    )
    recv = lax.all_to_all(send, "tensor", split_axis=0, concat_axis=0, tiled=True)
    routed = call(
        functools.partial(clean_kernel, rows, peers, slabs, feats),
        (recv, side),
        "vv",
        sds((slabs * 8, 128), BF16),
        [],
        10**7,
        10**6,
        8,
    )
    landed = lax.all_to_all(routed, "wide", split_axis=0, concat_axis=0, tiled=True)
    width = 128 * (((rows + 2) // 2 + 1) // 2)
    copies = call(
        functools.partial(pick_kernel, rows, peers, slabs),
        (here, landed),
        "sv",
        sds((peers * 8, width), BF16),
        [pltpu.VMEM((slabs * 8, 128), F32)],
        10**6,
        10**6,
        8,
    )
    latents = lax.all_to_all(copies, "tensor", split_axis=0, concat_axis=0, tiled=True)
    own = lax.dynamic_slice_in_dim(conv1_weight, t * outs, outs, 2)
    w1 = own.transpose(0, 2, 1).reshape(9 * outs, -1)
    b1 = jnp.broadcast_to(lax.dynamic_slice_in_dim(conv1_bias, t * outs, outs, 0)[:, None], (outs, 128))
    weight, bias = gather_call(here, recv, peers, outs)
    return decode_call(rows, here, latents, weight, bias, w1, b1)


def solution(mesh):
    return jax.shard_map(
        shards,
        mesh=mesh,
        in_specs=(
            P("wide", "tensor"),
            P(None, "tensor"),
            P("tensor", None),
            P("wide", None),
            P(),
            P("wide"),
            P(None, "tensor"),
            P("tensor"),
            P(),
            P(),
        ),
        out_specs=(P("wide", "tensor", None), P("wide", "tensor", None)),
        check_vma=False,
    )
```

time: 102 us -> 88.9 us (0.87)
  blocking collectives: 38.5 us -> 56 us
  waiting for transfers between devices: 16.5 us -> 5.02 us
  starting transfers between devices: 11.9 us -> 3.7 us
  Pallas kernels: 25.1 us -> 17.4 us
  local copies, waits for them, and re-layouts: 8.42 us -> 3.64 us
  other arithmetic: 0.08 us -> 1.32 us
    all_to_all x0 -> x1, blocking collectives: none -> 18 us  [shards(): lax.all_to_all(send, 'tensor', split_axis=0, concat_axis=0, tiled=True)]
    all_to_all x1 -> x0, waiting for transfers between devices: 10 us -> none  [shards(): lax.all_to_all(send, 'tensor', split_axis=0, concat_axis=0, tiled=True)]
    all_to_all x1 -> x0, starting transfers between devices: 7.99 us -> none  [shards(): lax.all_to_all(send, 'tensor', split_axis=0, concat_axis=0, tiled=True)]
    pallas_call x4 -> x5, Pallas kernels: 25.1 us -> 17.4 us  [call(): pl.pallas_call(body, out_shape=out_shape, in_specs=[pl.BlockSpec(memory_s...]
    unnamed x16 -> x4, local copies, waits for them, and re-layouts: 5.53 us -> 0.76 us
    all_to_all x1, waiting for transfers between devices: 6.49 us -> 5.02 us  [shards(): lax.all_to_all(copies, 'tensor', split_axis=0, concat_axis=0, tiled=True)]
    concatenate x0 -> x1, other arithmetic: none -> 1.32 us  [shards(): jnp.concatenate([jnp.stack([t, w]).astype(jnp.int32), step_index, slab_ta...]
  transfers between devices with their start and end apart: 2 -> 1, of which waited for: 2 -> 1; matrix products, arithmetic and copies ran while one was open for 3% -> 3% of each run, Pallas kernels for 0% -> 2%
where the time goes in v2:
time: 88.9 us; the launch traced here: 88.4 us
  blocking collectives  56 us (63%)
  Pallas kernels  17.4 us (20%)
  waiting for transfers between devices  5.02 us (6%)
  starting transfers between devices  3.7 us (4%)
  local copies, waits for them, and re-layouts  3.64 us (4%)
  other arithmetic  1.32 us (1%)
  between operations  1.32 us (1%)
    all_to_all x1, blocking collectives, shards(): lax.all_to_all(routed, 'wide', split_axis=0, concat_axis=0, tiled=True)  38 us
    all_to_all x1, blocking collectives, shards(): lax.all_to_all(send, 'tensor', split_axis=0, concat_axis=0, tiled=True)  18 us
    pallas_call x5, Pallas kernels, call(): pl.pallas_call(body, out_shape=out_shape, in_specs=[pl.BlockSpec(memory_s...  17.4 us
    all_to_all x1, waiting for transfers between devices, shards(): lax.all_to_all(copies, 'tensor', split_axis=0, concat_axis=0, tiled=True)  5.02 us
    all_to_all x1, starting transfers between devices, shards(): lax.all_to_all(copies, 'tensor', split_axis=0, concat_axis=0, tiled=True)  3.7 us
    transpose x2, local copies, waits for them, and re-layouts, shards(): w1 = own.transpose(0, 2, 1).reshape(9 * outs, -1)  2.05 us
  transfers between devices with their start and end apart: 1, of which 1 were waited for; matrix products, arithmetic and copies ran while one was open for 3% of the time, Pallas kernels for 2%

profile of v2, /device:TPU:1, one launch (start us, length us, event | category | flops | bytes accessed | tf_op | source)
XLA Modules:
  0.0 88.4 jit_solution(3835847596730304632)
XLA Ops:
  1.3 1.3 %pad_add_fusion.here = s32[27]{0:T(128)} fusion(s32[24]{0:T(128)} %param.15, s32[1]{0:T(128)S(6)} %copy.13, s32[1]{0:T(128)} %bitcast.1, s32[1]{0:T(128)} %bitcast), kind=kLoop, calls=%fused_computation.1 | loop fusion | flops 81 | bytes 216 | tf_op jit(solution)/shard_map/concatenate | solution.py:393
  2.6 0.0 copy-start.1
  2.6 3.9 %shard_map.113 = (bf16[1536,128]{1,0:T(8,128)(2,1)}, f32[64,128]{1,0:T(8,128)}) custom-call(s32[27]{0:T(128)} %pad_add_fusion.here, bf16[192,1536]{1,0:T(8,128)(2,1)} %bitcast.23, f32[64,1536]{1,0:T(8,128)} %bitcast.24, f32[2,192]{1,0:T(2,128)} %rest_0_.1, bf16[64,192]{1,0:T(8,128)(2,1)} %bitcast.25, bf16[32,144]{1,0:T(8,128)(2,1)} %bitcast.26, f32[1,32]{1,0:T(1,128)} %bitcast.27), custom_call_target="tpu_custom_call" | custom-call | flops 1000000000 | bytes 2000000 | tf_op jit(solution)/shard_map/pallas_call | solution.py:328
  6.5 18.0 %all_to_all.33 = bf16[16,96,128]{2,1,0:T(8,128)(2,1)S(1)} all-to-all(bf16[16,96,128]{2,1,0:T(8,128)(2,1)} %bitcast.22), channel_id=1, replica_groups=mesh['wide'=48,'tensor'=16] {'tensor'}, dimensions={0} | all-to-all | bytes 786432 | tf_op jit(solution)/shard_map/all_to_all | solution.py:412
  24.5 0.0 copy-start
  24.5 0.8 copy-done
  25.3 1.1 %shard_map.114 = bf16[384,128]{1,0:T(8,128)(2,1)S(1)} custom-call(bf16[1536,128]{1,0:T(8,128)(2,1)S(1)} %bitcast.16, f32[64,128]{1,0:T(8,128)S(1)} %copy-done), custom_call_target="tpu_custom_call" | custom-call | flops 10000000 | bytes 1000000 | tf_op jit(solution)/shard_map/pallas_call | solution.py:328
  26.3 38.0 %all_to_all.34 = bf16[48,8,128]{2,1,0:T(8,128)(2,1)S(1)} all-to-all(bf16[48,8,128]{2,1,0:T(8,128)(2,1)S(1)} %bitcast.18), channel_id=1, replica_groups=mesh['wide'=48,'tensor'=16] {'wide'}, dimensions={0} | all-to-all | bytes 196608 | tf_op jit(solution)/shard_map/all_to_all | solution.py:423
  64.4 0.0 copy-done.1
  64.4 1.4 %shard_map.115 = bf16[128,896]{1,0:T(8,128)(2,1)} custom-call(s32[27]{0:T(128)S(1)} %copy-done.1, bf16[384,128]{1,0:T(8,128)(2,1)S(1)} %bitcast.19), custom_call_target="tpu_custom_call" | custom-call | flops 1000000 | bytes 1000000 | tf_op jit(solution)/shard_map/pallas_call | solution.py:328
  65.8 3.7 %all-to-all-start.2 = ((bf16[16,8,896]{2,1,0:T(8,128)(2,1)}), bf16[16,8,896]{2,1,0:T(8,128)(2,1)S(1)}, u32[]{:S(2)}, u32[]{:S(2)}) async-start(bf16[16,8,896]{2,1,0:T(8,128)(2,1)} %bitcast.11), calls=%async_computation.2 | async-start | bytes 458752 | tf_op jit(solution)/shard_map/all_to_all | solution.py:435
  69.5 1.7 %dynamic-slice_bitcast_fusion = bf16[9,32,512]{1,2,0:T(8,128)(2,1)S(1)} fusion(bf16[9,512,512]{2,1,0:T(8,128)(2,1)} %param.18, s32[]{:T(128)S(6)} %select_n.4), kind=kLoop, calls=%fused_computation | loop fusion | bytes 589828 | tf_op jit(solution)/shard_map/transpose | solution.py:437
  71.1 0.4 copy.12
  71.5 0.8 dynamic_slice.7
  72.3 1.5 %shard_map.116 = (bf16[544,144]{1,0:T(8,128)(2,1)S(1)}, f32[544,128]{1,0:T(8,128)S(1)}) custom-call(s32[27]{0:T(128)S(1)} %copy-done.1, bf16[1536,128]{1,0:T(8,128)(2,1)S(1)} %bitcast.17), custom_call_target="tpu_custom_call" | custom-call | flops 1000000 | bytes 1000000 | tf_op jit(solution)/shard_map/pallas_call | solution.py:328
  73.8 5.0 %all-to-all-done.2 = bf16[16,8,896]{2,1,0:T(8,128)(2,1)S(1)} async-done(((bf16[16,8,896]{2,1,0:T(8,128)(2,1)}), bf16[16,8,896]{2,1,0:T(8,128)(2,1)S(1)}, u32[]{:S(2)}, u32[]{:S(2)}) %all-to-all-start.2) | async-done | bytes 229408 | tf_op jit(solution)/shard_map/all_to_all | solution.py:435
  78.8 0.1 broadcast_in_dim.2.b1_ref
  78.8 9.6 %shard_map.117 = (bf16[48,32,128]{2,1,0:T(8,128)(2,1)}, bf16[48,32,128]{2,1,0:T(8,128)(2,1)}) custom-call(s32[27]{0:T(128)S(1)} %copy-done.1, bf16[128,896]{1,0:T(8,128)(2,1)S(1)} %bitcast.21, bf16[544,144]{1,0:T(8,128)(2,1)S(1)} %get-tuple-element.8.weight, f32[544,128]{1,0:T(8,128)S(1)} %get-tuple-element.9.bias, bf16[288,512]{1,0:T(8,128)(2,1)S(1)} %bitcast.20, ...), custom_call_target="tpu_custom_call" | custom-call | flops 6000000000 | bytes 3000000 | tf_op jit(solution)/shard_map/pallas_call | solution.py:328
Async XLA Ops:
  2.6 61.8 %copy-start.1 = (s32[27]{0:T(128)S(1)}, s32[27]{0:T(128)}, u32[]{:S(2)}) copy-start(s32[27]{0:T(128)} %pad_add_fusion.here) | copy-start | bytes 328
  24.5 0.8 copy-start
  65.8 13.0 %all-to-all-start.2 = ((bf16[16,8,896]{2,1,0:T(8,128)(2,1)}), bf16[16,8,896]{2,1,0:T(8,128)(2,1)S(1)}, u32[]{:S(2)}, u32[]{:S(2)}) async-start(bf16[16,8,896]{2,1,0:T(8,128)(2,1)} %bitcast.11), calls=%async_computation.2 | async-start | bytes 458752 | tf_op jit(solution)/shard_map/all_to_all | solution.py:435

commit v3 on v2

--- a/solution.py
+++ b/solution.py
@@ -45,14 +45,15 @@
     return jnp.sum(jnp.where(iota((n, n), 0) == iota((n, n), 1), column, 0.0), axis=0, keepdims=True)
 
 
-def project_kernel(rows, peers, here, h_hbm, noisy_hbm, *rest):
+def project_kernel(rows, peers, h_hbm, *rest):
     small = rest[:4]
-    send_ref, side_ref, h_ref, noisy_ref, mod_ref, w_ref, win_ref, bin_ref, sums, drawn, sems = rest[4:]
-    moves = zip((h_hbm, *small, noisy_hbm), (h_ref, mod_ref, w_ref, win_ref, bin_ref, noisy_ref))
+    send_ref, h_ref, mod_ref, w_ref, win_ref, bin_ref, sums, sems = rest[4:]
+    moves = list(zip(small, (mod_ref, w_ref, win_ref, bin_ref)))
+    moves.append((h_hbm, h_ref))
     copies = [pltpu.make_async_copy(src, dst, sems.at[n]) for n, (src, dst) in enumerate(moves)]
     for copy in copies:
         copy.start()
-    for copy in copies[1:5]:
+    for copy in copies[:4]:
         copy.wait()
     per = GRID // peers
     feats = h_ref.shape[0]
@@ -64,7 +65,7 @@
     lane = iota((1, 128), 1)
     low = lane < 64
     step = 256
-    copies[0].wait()
+    copies[4].wait()
     for at in range(0, h_ref.shape[1], step):
         hid = h_ref[:, at : at + step]
         prod = jnp.dot(left, hid, preferred_element_type=F32)
@@ -106,6 +107,12 @@
             tile = tile + (pltpu.roll(stat[8 * g : 8 * g + 8, :], 24 * g, 1) if g else stat[:8, :])
         send_ref[base + STAT : base + STAT + 16, :] = jnp.concatenate([tile, lower], axis=0).astype(BF16)
         send_ref[base + WROW : base + WROW + 32, :] = main_w
+
+
+def side_kernel(rows, peers, here, noisy_ref, side_ref, drawn):
+    per = GRID // peers
+    lane = iota((1, 128), 1)
+    fill = [jnp.zeros((SR - rows, 128), F32)] if rows < SR else []
     owner = jnp.full((8, 128), -9, jnp.int32)
     for j in range(rows):
         owner = jnp.where((lane % SR == j) & (lane < 4 * SR), here[3 + j], owner)
@@ -113,9 +120,8 @@
     sigma = shift_value * frac / (1.0 + (shift_value - 1.0) * frac)
     side_ref[2 * SR : 2 * SR + 8, :] = owner.astype(F32)
     side_ref[2 * SR + 8 : 2 * SR + 16, :] = sigma
-    copies[5].wait()
-    for at in range(0, h_ref.shape[1], step):
-        drawn[at : at + step, :] = jnp.transpose(noisy_ref[:, at : at + step])
+    for at in range(0, noisy_ref.shape[1], 256):
+        drawn[at : at + 256, :] = jnp.transpose(noisy_ref[:, at : at + 256])
     mine = here[0] * per
     for half in range(per // 2):
         one = drawn[pl.ds(mine + 2 * half, rows, stride=GRID), :]
@@ -244,7 +250,7 @@
     load(here[0] * BLOCK, peers * outs)
 
 
-def decode_kernel(rows, here, lat_ref, weight, bias, w1_ref, b1_ref, dec_ref, res_ref, spread_out, shifted, act, act2, taps):
+def decode_kernel(rows, here, lat_ref, weight, bias, w1_ref, b1_ref, dec_ref, res_ref, spread_out, shifted, act, act2, tap0, tap1, tap2, tap3):
     slab_height = 2 * rows
     first_row = here[1] * slab_height
     count = rows + 2
@@ -288,37 +294,42 @@
         halved = 0.5 * value
         buf[...] = (halved + halved * jnp.tanh(halved)).astype(BF16)
 
-    def multiply(m, buf):
+    def multiply(m, buf, slot):
         tap = jnp.dot(w1_ref[...], buf[...], preferred_element_type=F32)
-        taps[2 * m] = tap[:, :128]
-        taps[2 * m + 1] = tap[:, 128:]
-
-    def finish(m):
-        for y in (2 * m - 2, 2 * m - 1):
+        slot[0] = tap[:, :128]
+        slot[1] = tap[:, 128:]
+
+    def finish(m, before, slot):
+        lines = (before.at[0], before.at[1], slot.at[0], slot.at[1])
+        for n in range(2):
+            y = 2 * m - 2 + n
             global_row = lax.rem(first_row + y, WPIX)
-            sums = taps[y + 1, 3 * outs : 6 * outs, :]
-            sums = sums + jnp.where(global_row != 0, taps[y, 0 : 3 * outs, :], 0.0)
-            sums = sums + jnp.where(global_row != WPIX - 1, taps[y + 2, 6 * outs :, :], 0.0)
+            sums = lines[n + 1][3 * outs : 6 * outs, :]
+            sums = sums + jnp.where(global_row != 0, lines[n][0 : 3 * outs, :], 0.0)
+            sums = sums + jnp.where(global_row != WPIX - 1, lines[n + 2][6 * outs :, :], 0.0)
             total = sums[outs : 2 * outs, :] + b1_ref[...]
             total = total + jnp.where(lane == 0, 0.0, pltpu.roll(sums[0:outs, :], 1, 1))
             total = total + jnp.where(lane == 127, 0.0, pltpu.roll(sums[2 * outs :, :], 127, 1))
             res_ref[y] = total.astype(BF16)
 
+    acts = (act, act2)
     features(0, act)
-    taps[0:4] = jnp.zeros((4, 9 * outs, 128), F32)
-
-    def double(step, carry):
-        for n, (now, before) in enumerate(((act2, act), (act, act2))):
-            m = 2 * step + 1 + n
-            features(m, now)
-            multiply(m - 1, before)
-            finish(jnp.maximum(m - 2, 1))
+    tap2[...] = jnp.zeros_like(tap2)
+    tap3[...] = jnp.zeros_like(tap3)
+    taps = (tap0, tap1, tap2, tap3)
+
+    def several(step, carry):
+        for n in range(12):
+            m = 12 * step + 1 + n
+            finish(jnp.maximum(m - 2, 1), taps[(n + 2) % 4], taps[(n + 3) % 4])
+            features(m, acts[(n + 1) % 2])
+            multiply(m - 1, acts[n % 2], taps[n % 4])
         return carry
 
-    lax.fori_loop(0, rows // 2, double, 0)
-    multiply(rows, act)
-    finish(rows - 1)
-    finish(rows)
+    lax.fori_loop(0, rows // 12, several, 0)
+    finish(rows - 1, taps[(rows - 2) % 4], taps[(rows - 1) % 4])
+    multiply(rows, acts[rows % 2], taps[rows % 4])
+    finish(rows, taps[(rows - 1) % 4], taps[rows % 4])
 
 
 SPACES = {"s": pltpu.SMEM, "v": pltpu.VMEM, "h": pltpu.HBM}
@@ -351,8 +362,8 @@
             pltpu.VMEM((2 * (rows + 2) * 48, 128), BF16),
             pltpu.VMEM((channels, 256), BF16),
             pltpu.VMEM((channels, 256), BF16),
-            pltpu.VMEM((2 * rows + 2, 9 * outs, 128), F32),
-        ],
+        ]
+        + [pltpu.VMEM((2, 9 * outs, 128), F32)] * 4,
         6 * 10**9,
         3 * 10**6,
         24,
@@ -368,6 +379,48 @@
         "sv",
         (sds((many, 144), BF16), sds((many, 128), F32)),
         [],
+        10**6,
+        10**6,
+        8,
+    )
+
+
+def project_call(rows, peers, hidden, small):
+    large = (hidden,) + small
+    return call(
+        functools.partial(project_kernel, rows, peers),
+        large,
+        "hhhhh",
+        jax.ShapeDtypeStruct((peers * BLOCK, 128), BF16),
+        [pltpu.VMEM(x.shape, x.dtype) for x in large]
+        + [pltpu.VMEM((hidden.shape[1], 128), F32), pltpu.SemaphoreType.DMA((5,))],
+        10**9,
+        2 * 10**6,
+        60,
+    )
+
+
+def clean_call(rows, peers, slabs, feats, recv, side):
+    return call(
+        functools.partial(clean_kernel, rows, peers, slabs, feats),
+        (recv, side),
+        "vv",
+        jax.ShapeDtypeStruct((slabs * 8, 128), BF16),
+        [],
+        10**7,
+        10**6,
+        8,
+    )
+
+
+def pick_call(rows, peers, slabs, here, landed):
+    width = 128 * (((rows + 2) // 2 + 1) // 2)
+    return call(
+        functools.partial(pick_kernel, rows, peers, slabs),
+        (here, landed),
+        "sv",
+        jax.ShapeDtypeStruct((peers * 8, width), BF16),
+        [pltpu.VMEM((slabs * 8, 128), F32)],
         10**6,
         10**6,
         8,
@@ -392,46 +445,25 @@
     w = lax.axis_index("wide")
     here = jnp.concatenate([jnp.stack([t, w]).astype(jnp.int32), step_index, slab_table])
     rows = slab_table.shape[0]
-    tokens, feats = hidden.shape
+    feats = hidden.shape[1]
     outs = conv_in_weight.shape[1]
     sds = jax.ShapeDtypeStruct
-    large = (hidden.T, noisy.T)
     small = (modulation, final_weight.T, conv_in_weight.T, conv_in_bias.reshape(1, -1))
-
-    send, side = call(
-        functools.partial(project_kernel, rows, peers),
-        (here, hidden.T, noisy.T, *small),
-        "shhhhhh",
-        (sds((peers * BLOCK, 128), BF16), sds((2 * SR + 16, 128), F32)),
-        [pltpu.VMEM(x.shape, x.dtype) for x in large + small]
-        + [pltpu.VMEM((tokens, 128), F32), pltpu.VMEM((tokens, noisy.shape[1]), F32), pltpu.SemaphoreType.DMA((6,))],
-        10**9,
-        2 * 10**6,
-        60,
+    send = project_call(rows, peers, hidden.T, small)
+    side = call(
+        functools.partial(side_kernel, rows, peers),
+        (here, noisy.T),
+        "sv",
+        sds((2 * SR + 16, 128), F32),
+        [pltpu.VMEM(noisy.shape, F32)],
+        10**6,
+        10**6,
+        8,
     )
     recv = lax.all_to_all(send, "tensor", split_axis=0, concat_axis=0, tiled=True)
-    routed = call(
-        functools.partial(clean_kernel, rows, peers, slabs, feats),
-        (recv, side),
-        "vv",
-        sds((slabs * 8, 128), BF16),
-        [],
-        10**7,
-        10**6,
-        8,
-    )
+    routed = clean_call(rows, peers, slabs, feats, recv, side)
     landed = lax.all_to_all(routed, "wide", split_axis=0, concat_axis=0, tiled=True)
-    width = 128 * (((rows + 2) // 2 + 1) // 2)
-    copies = call(
-        functools.partial(pick_kernel, rows, peers, slabs),
-        (here, landed),
-        "sv",
-        sds((peers * 8, width), BF16),
-        [pltpu.VMEM((slabs * 8, 128), F32)],
-        10**6,
-        10**6,
-        8,
-    )
+    copies = pick_call(rows, peers, slabs, here, landed)
     latents = lax.all_to_all(copies, "tensor", split_axis=0, concat_axis=0, tiled=True)
     own = lax.dynamic_slice_in_dim(conv1_weight, t * outs, outs, 2)
     w1 = own.transpose(0, 2, 1).reshape(9 * outs, -1)

time: 88.9 us -> 82.1 us (0.924)
  blocking collectives: 56 us -> 38 us
  starting transfers between devices: 3.7 us -> 11.7 us
  waiting for transfers between devices: 5.02 us -> 12.7 us
  Pallas kernels: 17.4 us -> 14.3 us
    all_to_all x1 -> x0, blocking collectives: 18 us -> none  [shards(): lax.all_to_all(send, 'tensor', split_axis=0, concat_axis=0, tiled=True)]
    all_to_all x0 -> x1, starting transfers between devices: none -> 8 us  [shards(): lax.all_to_all(send, 'tensor', split_axis=0, concat_axis=0, tiled=True)]
    all_to_all x0 -> x1, waiting for transfers between devices: none -> 7.7 us  [shards(): lax.all_to_all(send, 'tensor', split_axis=0, concat_axis=0, tiled=True)]
    pallas_call x5 -> x6, Pallas kernels: 17.4 us -> 14.3 us  [call(): pl.pallas_call(body, out_shape=out_shape, in_specs=[pl.BlockSpec(memory_s...]
  transfers between devices with their start and end apart: 1 -> 2, of which waited for: 1 -> 2; matrix products, arithmetic and copies ran while one was open for 3% -> 4% of each run, Pallas kernels for 2% -> 3%
where the time goes in v3:
time: 82.1 us; the launch traced here: 81.7 us
  blocking collectives  38 us (46%)
  Pallas kernels  14.3 us (17%)
  waiting for transfers between devices  12.7 us (15%)
  starting transfers between devices  11.7 us (14%)
  local copies, waits for them, and re-layouts  2.88 us (4%)
  between operations  1.34 us (2%)
    all_to_all x1, blocking collectives, shards(): lax.all_to_all(routed, 'wide', split_axis=0, concat_axis=0, tiled=True)  38 us
    pallas_call x6, Pallas kernels, call(): pl.pallas_call(body, out_shape=out_shape, in_specs=[pl.BlockSpec(memory_s...  14.3 us
    all_to_all x1, starting transfers between devices, shards(): lax.all_to_all(send, 'tensor', split_axis=0, concat_axis=0, tiled=True)  8 us
    all_to_all x1, waiting for transfers between devices, shards(): lax.all_to_all(send, 'tensor', split_axis=0, concat_axis=0, tiled=True)  7.7 us
    all_to_all x1, waiting for transfers between devices, shards(): lax.all_to_all(copies, 'tensor', split_axis=0, concat_axis=0, tiled=True)  5.02 us
    all_to_all x1, starting transfers between devices, shards(): lax.all_to_all(copies, 'tensor', split_axis=0, concat_axis=0, tiled=True)  3.7 us
    transpose x2, local copies, waits for them, and re-layouts, shards(): w1 = own.transpose(0, 2, 1).reshape(9 * outs, -1)  2.05 us
  transfers between devices with their start and end apart: 2, of which 2 were waited for; matrix products, arithmetic and copies ran while one was open for 4% of the time, Pallas kernels for 3%

profile of v3, /device:TPU:1, one launch (start us, length us, event | category | flops | bytes accessed | tf_op | source)
XLA Modules:
  0.0 81.7 jit_solution(12624410840505430716)
XLA Ops:
  0.6 0.0 copy-start
  0.6 3.0 %shard_map.113 = bf16[1536,128]{1,0:T(8,128)(2,1)} custom-call(bf16[192,1536]{1,0:T(8,128)(2,1)} %bitcast.24, f32[2,192]{1,0:T(2,128)} %rest_0_.1, bf16[64,192]{1,0:T(8,128)(2,1)} %bitcast.25, bf16[32,144]{1,0:T(8,128)(2,1)} %bitcast.26, f32[1,32]{1,0:T(1,128)} %bitcast.27), custom_call_target="tpu_custom_call" | custom-call | flops 1000000000 | bytes 2000000 | tf_op jit(solution)/shard_map/pallas_call | solution.py:339
  3.6 8.0 %all-to-all-start = ((bf16[16,96,128]{2,1,0:T(8,128)(2,1)}), bf16[16,96,128]{2,1,0:T(8,128)(2,1)S(1)}, u32[]{:S(2)}, u32[]{:S(2)}) async-start(bf16[16,96,128]{2,1,0:T(8,128)(2,1)} %bitcast.23), calls=%async_computation | async-start | bytes 786432 | tf_op jit(solution)/shard_map/all_to_all | solution.py:463
  12.3 0.7 pad_add_fusion.here
  13.0 0.0 copy-done
  13.0 0.9 %shard_map.114.side_ref = f32[64,128]{1,0:T(8,128)S(1)} custom-call(s32[27]{0:T(128)S(1)} %pad_add_fusion.here, f32[64,1536]{1,0:T(8,128)S(1)} %bitcast.19), custom_call_target="tpu_custom_call" | custom-call | flops 1000000 | bytes 1000000 | tf_op jit(solution)/shard_map/pallas_call | solution.py:339
  13.9 7.7 %all-to-all-done = bf16[16,96,128]{2,1,0:T(8,128)(2,1)S(1)} async-done(((bf16[16,96,128]{2,1,0:T(8,128)(2,1)}), bf16[16,96,128]{2,1,0:T(8,128)(2,1)S(1)}, u32[]{:S(2)}, u32[]{:S(2)}) %all-to-all-start) | async-done | bytes 393248 | tf_op jit(solution)/shard_map/all_to_all | solution.py:463
  21.6 1.0 %shard_map.115 = bf16[384,128]{1,0:T(8,128)(2,1)S(1)} custom-call(bf16[1536,128]{1,0:T(8,128)(2,1)S(1)} %bitcast.16, f32[64,128]{1,0:T(8,128)S(1)} %shard_map.114.side_ref), custom_call_target="tpu_custom_call" | custom-call | flops 10000000 | bytes 1000000 | tf_op jit(solution)/shard_map/pallas_call | solution.py:339
  22.7 38.0 %all_to_all.33 = bf16[48,8,128]{2,1,0:T(8,128)(2,1)S(1)} all-to-all(bf16[48,8,128]{2,1,0:T(8,128)(2,1)S(1)} %bitcast.18), channel_id=1, replica_groups=mesh['wide'=48,'tensor'=16] {'wide'}, dimensions={0} | all-to-all | bytes 196608 | tf_op jit(solution)/shard_map/all_to_all | solution.py:465
  60.7 1.4 %shard_map.116 = bf16[128,896]{1,0:T(8,128)(2,1)} custom-call(s32[27]{0:T(128)S(1)} %pad_add_fusion.here, bf16[384,128]{1,0:T(8,128)(2,1)S(1)} %bitcast.20), custom_call_target="tpu_custom_call" | custom-call | flops 1000000 | bytes 1000000 | tf_op jit(solution)/shard_map/pallas_call | solution.py:339
  62.1 3.7 %all-to-all-start.2 = ((bf16[16,8,896]{2,1,0:T(8,128)(2,1)}), bf16[16,8,896]{2,1,0:T(8,128)(2,1)S(1)}, u32[]{:S(2)}, u32[]{:S(2)}) async-start(bf16[16,8,896]{2,1,0:T(8,128)(2,1)} %bitcast.11), calls=%async_computation.2 | async-start | bytes 458752 | tf_op jit(solution)/shard_map/all_to_all | solution.py:467
  65.8 1.7 %dynamic-slice_bitcast_fusion = bf16[9,32,512]{1,2,0:T(8,128)(2,1)S(1)} fusion(bf16[9,512,512]{2,1,0:T(8,128)(2,1)} %param.18, s32[]{:T(128)S(6)} %select_n.4), kind=kLoop, calls=%fused_computation | loop fusion | bytes 589828 | tf_op jit(solution)/shard_map/transpose | solution.py:469
  67.5 0.4 copy.12
  67.8 0.8 dynamic_slice.7
  68.6 1.5 %shard_map.117 = (bf16[544,144]{1,0:T(8,128)(2,1)S(1)}, f32[544,128]{1,0:T(8,128)S(1)}) custom-call(s32[27]{0:T(128)S(1)} %pad_add_fusion.here, bf16[1536,128]{1,0:T(8,128)(2,1)S(1)} %bitcast.17), custom_call_target="tpu_custom_call" | custom-call | flops 1000000 | bytes 1000000 | tf_op jit(solution)/shard_map/pallas_call | solution.py:339
  70.1 5.0 %all-to-all-done.2 = bf16[16,8,896]{2,1,0:T(8,128)(2,1)S(1)} async-done(((bf16[16,8,896]{2,1,0:T(8,128)(2,1)}), bf16[16,8,896]{2,1,0:T(8,128)(2,1)S(1)}, u32[]{:S(2)}, u32[]{:S(2)}) %all-to-all-start.2) | async-done | bytes 229408 | tf_op jit(solution)/shard_map/all_to_all | solution.py:467
  75.1 0.1 broadcast_in_dim.2.b1_ref
  75.2 6.5 %shard_map.118 = (bf16[48,32,128]{2,1,0:T(8,128)(2,1)}, bf16[48,32,128]{2,1,0:T(8,128)(2,1)}) custom-call(s32[27]{0:T(128)S(1)} %pad_add_fusion.here, bf16[128,896]{1,0:T(8,128)(2,1)S(1)} %bitcast.22, bf16[544,144]{1,0:T(8,128)(2,1)S(1)} %get-tuple-element.4.weight, f32[544,128]{1,0:T(8,128)S(1)} %get-tuple-element.5.bias, bf16[288,512]{1,0:T(8,128)(2,1)S(1)} %bitcast.21, ...), custom_call_target="tpu_custom_call" | custom-call | flops 6000000000 | bytes 3000000 | tf_op jit(solution)/shard_map/pallas_call | solution.py:339
Async XLA Ops:
  0.6 12.4 %copy-start = (f32[1536,64]{0,1:T(8,128)S(1)}, f32[1536,64]{0,1:T(8,128)}, u32[]{:S(2)}) copy-start(f32[1536,64]{0,1:T(8,128)} %param.13) | copy-start | bytes 1179652
  3.6 18.0 %all-to-all-start = ((bf16[16,96,128]{2,1,0:T(8,128)(2,1)}), bf16[16,96,128]{2,1,0:T(8,128)(2,1)S(1)}, u32[]{:S(2)}, u32[]{:S(2)}) async-start(bf16[16,96,128]{2,1,0:T(8,128)(2,1)} %bitcast.23), calls=%async_computation | async-start | bytes 786432 | tf_op jit(solution)/shard_map/all_to_all | solution.py:463
  62.1 13.0 %all-to-all-start.2 = ((bf16[16,8,896]{2,1,0:T(8,128)(2,1)}), bf16[16,8,896]{2,1,0:T(8,128)(2,1)S(1)}, u32[]{:S(2)}, u32[]{:S(2)}) async-start(bf16[16,8,896]{2,1,0:T(8,128)(2,1)} %bitcast.11), calls=%async_computation.2 | async-start | bytes 458752 | tf_op jit(solution)/shard_map/all_to_all | solution.py:467

commit v4 on v3

--- a/solution.py
+++ b/solution.py
@@ -109,17 +109,33 @@
         send_ref[base + WROW : base + WROW + 32, :] = main_w
 
 
-def side_kernel(rows, peers, here, noisy_ref, side_ref, drawn):
+def side_kernel(rows, peers, slabs, here, noisy_ref, side_ref, route_ref, choose_ref, drawn):
     per = GRID // peers
     lane = iota((1, 128), 1)
     fill = [jnp.zeros((SR - rows, 128), F32)] if rows < SR else []
-    owner = jnp.full((8, 128), -9, jnp.int32)
+    owner = jnp.full((1, 128), -9, jnp.int32)
     for j in range(rows):
         owner = jnp.where((lane % SR == j) & (lane < 4 * SR), here[3 + j], owner)
+    shape = (slabs * 8, 128)
+    row = iota(shape, 0)
+    col = iota(shape, 1)
+    slab = row // 8
+    upper = row % 8 < 4
+    dk = row % 4
+    turned = col // (2 * SR)
+    half = (col // SR) % 2
+    j = col % SR
+    right_half = half == dk // 2
+    target = jnp.where(upper, owner, jnp.where(j == 0, owner - 1, -9))
+    own = target == slab
+    take_low = (right_half & (turned == dk % 2) & own).astype(F32).astype(BF16)
+    above = upper & (j == rows - 1) & (owner + 1 == slab) & (owner >= 0)
+    take_high = (right_half & (turned == 1 - dk % 2) & above).astype(F32).astype(BF16)
+    route_ref[: slabs * 8, :] = take_low
+    route_ref[slabs * 8 :, :] = take_high
     frac = (jnp.zeros((8, 128), F32) + here[2].astype(F32)) / STEPS
     sigma = shift_value * frac / (1.0 + (shift_value - 1.0) * frac)
-    side_ref[2 * SR : 2 * SR + 8, :] = owner.astype(F32)
-    side_ref[2 * SR + 8 : 2 * SR + 16, :] = sigma
+    side_ref[2 * SR :, :] = sigma
     for at in range(0, noisy_ref.shape[1], 256):
         drawn[at : at + 256, :] = jnp.transpose(noisy_ref[:, at : at + 256])
     mine = here[0] * per
@@ -129,6 +145,31 @@
         both = jnp.concatenate([one, two], axis=1)
         side_ref[half * SR : (half + 1) * SR, :] = jnp.concatenate([both] + fill, axis=0) if fill else both
 
+    count = rows + 2
+    half_rows = count // 2
+    blocks = (half_rows + 1) // 2
+    row = iota((blocks * 8, 128), 0)
+    picked = [jnp.full((blocks * 8, 128), -1, jnp.int32) for _ in range(4)]
+
+    def source(j):
+        return lax.rem(2 * here[1] - here[3 + j] + 2 * slabs, slabs)
+
+    for i in range(count):
+        n = i % half_rows
+        if i == 0:
+            at, is_low = (lax.rem(source(rows - 1) - 1 + slabs, slabs) * 8, False)
+        elif i == count - 1:
+            at, is_low = (lax.rem(source(0) + 1, slabs) * 8 + 4, True)
+        else:
+            at, is_low = (source(i - 1) * 8, True)
+        group = (0 if is_low else 1) if n % 2 == 0 else (2 if is_low else 3)
+        mine = row // 4 == 2 * (n // 2) + i // half_rows
+        picked[group] = jnp.where(mine, at + row % 4, picked[group])
+    wanted = jnp.concatenate(picked, axis=0)
+    column = iota((1, 128), 1)
+    for at in range(0, slabs * 8, 128):
+        choose_ref[:, at : at + 128] = (wanted == column + at).astype(F32).astype(BF16)
+
 
 def spread(tile, at, low):
     parts = []
@@ -139,7 +180,7 @@
     return jnp.concatenate(parts, axis=0)
 
 
-def clean_kernel(rows, peers, slabs, feats, recv_ref, side_ref, send_ref):
+def clean_kernel(peers, feats, recv_ref, side_ref, route_ref, send_ref):
     lane = iota((1, 128), 1)
     low = lane < 64
     total = jnp.zeros((2 * SR, 128), F32)
@@ -167,66 +208,23 @@
     square = pltpu.roll(mean, 116, 1)
     rstd = 1.0 / jnp.sqrt(square - mean * mean + norm_eps)
     velocity = total * spread(rstd, 0, low) + shifted
-    sigma = side_ref[2 * SR + 8 : 2 * SR + 9, :]
+    sigma = side_ref[2 * SR : 2 * SR + 1, :]
     clean = (side_ref[: 2 * SR, :] - sigma * velocity).astype(BF16).astype(F32)
     held = jnp.concatenate([clean, pltpu.roll(clean, 64, 1), jnp.zeros((128 - 4 * SR, 128), F32)], axis=0).astype(BF16)
-    owner = side_ref[2 * SR : 2 * SR + 1, :].astype(jnp.int32)
-    shape = (slabs * 8, 128)
-    row = iota(shape, 0)
-    col = iota(shape, 1)
-    slab = row // 8
-    upper = row % 8 < 4
-    dk = row % 4
-    turned = col // (2 * SR)
-    half = (col // SR) % 2
-    j = col % SR
-    right_half = half == dk // 2
-    target = jnp.where(upper, owner, jnp.where(j == 0, owner - 1, -9))
-    own = target == slab
-    take_low = (right_half & (turned == dk % 2) & own).astype(F32).astype(BF16)
-    above = upper & (j == rows - 1) & (owner + 1 == slab) & (owner >= 0)
-    take_high = (right_half & (turned == 1 - dk % 2) & above).astype(F32).astype(BF16)
-    left = jnp.dot(take_low, held, preferred_element_type=F32)
-    right = jnp.dot(take_high, held, preferred_element_type=F32)
-    send_ref[...] = jnp.where(low, left, right).astype(BF16)
-
-
-def pick_kernel(rows, peers, slabs, here, recv_ref, send_ref, wide):
-    wide[...] = recv_ref[...].astype(F32)
-    lane = iota((8, 128), 1)
-    low = lane < 64
-    top = iota((8, 128), 0) < 4
-    count = rows + 2
-    per = count // 2
-
-    def source(j):
-        return lax.rem(2 * here[1] - here[3 + j] + 2 * slabs, slabs)
-
-    def piece(i, at_low, at_top):
-        if i == 0:
-            x, is_low, is_top = (lax.rem(source(rows - 1) - 1 + slabs, slabs), False, True)
-        elif i == count - 1:
-            x, is_low, is_top = (lax.rem(source(0) + 1, slabs), True, False)
-        else:
-            x, is_low, is_top = (source(i - 1), True, True)
-        tile = wide[pl.ds(pl.multiple_of(x * 8, 8), 8), :]
-        if is_low != at_low:
-            tile = pltpu.roll(tile, 64, 1)
-        if is_top != at_top:
-            tile = pltpu.roll(tile, 4, 0)
-        return tile
-
-    for block in range((per + 1) // 2):
-        quarters = []
-        for at_top in (True, False):
-            for at_low in (True, False):
-                n = 2 * block + (0 if at_low else 1)
-                if n < per:
-                    quarters.append(piece(n + (0 if at_top else per), at_low, at_top))
-                else:
-                    quarters.append(jnp.zeros((8, 128), F32))
-        tile = jnp.where(top, jnp.where(low, quarters[0], quarters[1]), jnp.where(low, quarters[2], quarters[3]))
-        tile = tile.astype(BF16)
+    both = jnp.dot(route_ref[...], held, preferred_element_type=F32)
+    count = both.shape[0] // 2
+    send_ref[...] = jnp.where(low, both[:count, :], both[count:, :]).astype(BF16)
+
+
+def pick_kernel(peers, choose_ref, recv_ref, send_ref):
+    low = iota((1, 128), 1) < 64
+    rows = jnp.dot(choose_ref[...], recv_ref[...], preferred_element_type=F32)
+    group = rows.shape[0] // 4
+    left = rows[:group, :] + pltpu.roll(rows[group : 2 * group, :], 64, 1)
+    right = pltpu.roll(rows[2 * group : 3 * group, :], 64, 1) + rows[3 * group :, :]
+    tiles = jnp.where(low, left, right).astype(BF16)
+    for block in range(group // 8):
+        tile = tiles[block * 8 : block * 8 + 8, :]
         for peer in range(peers):
             send_ref[peer * 8 : peer * 8 + 8, block * 128 : (block + 1) * 128] = tile
 
@@ -280,7 +278,7 @@
         for n in range(2):
             q = 2 * m + n
             global_row = lax.rem(first_row - 1 + q + WPIX, WPIX)
-            block = shifted[pl.ds(pl.multiple_of(q * 48, 16), 144), :]
+            block = shifted[q * 48 : q * 48 + 144, :]
             up = jnp.where(global_row != 0, block[:48, :], jnp.zeros((48, 128), BF16))
             down = jnp.where(global_row != WPIX - 1, block[96:, :], jnp.zeros((48, 128), BF16))
             parts.append(jnp.concatenate([up, block[48:96, :], down], axis=0))
@@ -288,8 +286,10 @@
         feat = jnp.dot(weight[...], right, preferred_element_type=F32)
         both = jnp.concatenate([bias[...], bias[...]], axis=1)
         feat = (feat + both).astype(BF16)
-        dec_ref[jnp.minimum(2 * m, slab_height - 1)] = feat[all_out:, 128:]
-        dec_ref[jnp.abs(2 * m - 1)] = feat[all_out:, :128]
+        if m > 0:
+            dec_ref[2 * m - 1] = feat[all_out:, :128]
+        if m < rows:
+            dec_ref[2 * m] = feat[all_out:, 128:]
         value = feat[:all_out, :].astype(F32)
         halved = 0.5 * value
         buf[...] = (halved + halved * jnp.tanh(halved)).astype(BF16)
@@ -313,20 +313,13 @@
             res_ref[y] = total.astype(BF16)
 
     acts = (act, act2)
+    taps = (tap0, tap1, tap2, tap3)
     features(0, act)
-    tap2[...] = jnp.zeros_like(tap2)
-    tap3[...] = jnp.zeros_like(tap3)
-    taps = (tap0, tap1, tap2, tap3)
-
-    def several(step, carry):
-        for n in range(12):
-            m = 12 * step + 1 + n
-            finish(jnp.maximum(m - 2, 1), taps[(n + 2) % 4], taps[(n + 3) % 4])
-            features(m, acts[(n + 1) % 2])
-            multiply(m - 1, acts[n % 2], taps[n % 4])
-        return carry
-
-    lax.fori_loop(0, rows // 12, several, 0)
+    for m in range(1, rows + 1):
+        if m > 2:
+            finish(m - 2, taps[(m + 1) % 4], taps[(m + 2) % 4])
+        features(m, acts[m % 2])
+        multiply(m - 1, acts[(m - 1) % 2], taps[(m - 1) % 4])
     finish(rows - 1, taps[(rows - 2) % 4], taps[(rows - 1) % 4])
     multiply(rows, acts[rows % 2], taps[rows % 4])
     finish(rows, taps[(rows - 1) % 4], taps[rows % 4])
@@ -400,11 +393,11 @@
     )
 
 
-def clean_call(rows, peers, slabs, feats, recv, side):
+def clean_call(peers, slabs, feats, recv, side, route):
     return call(
-        functools.partial(clean_kernel, rows, peers, slabs, feats),
-        (recv, side),
-        "vv",
+        functools.partial(clean_kernel, peers, feats),
+        (recv, side, route),
+        "vvv",
         jax.ShapeDtypeStruct((slabs * 8, 128), BF16),
         [],
         10**7,
@@ -413,15 +406,14 @@
     )
 
 
-def pick_call(rows, peers, slabs, here, landed):
-    width = 128 * (((rows + 2) // 2 + 1) // 2)
+def pick_call(peers, choose, landed):
     return call(
-        functools.partial(pick_kernel, rows, peers, slabs),
-        (here, landed),
-        "sv",
-        jax.ShapeDtypeStruct((peers * 8, width), BF16),
-        [pltpu.VMEM((slabs * 8, 128), F32)],
-        10**6,
+        functools.partial(pick_kernel, peers),
+        (choose, landed),
+        "vv",
+        jax.ShapeDtypeStruct((peers * 8, choose.shape[0] // 32 * 128), BF16),
+        [],
+        10**7,
         10**6,
         8,
     )
@@ -450,20 +442,21 @@
     sds = jax.ShapeDtypeStruct
     small = (modulation, final_weight.T, conv_in_weight.T, conv_in_bias.reshape(1, -1))
     send = project_call(rows, peers, hidden.T, small)
-    side = call(
-        functools.partial(side_kernel, rows, peers),
+    blocks = ((rows + 2) // 2 + 1) // 2
+    side, route, choose = call(
+        functools.partial(side_kernel, rows, peers, slabs),
         (here, noisy.T),
         "sv",
-        sds((2 * SR + 16, 128), F32),
+        (sds((2 * SR + 8, 128), F32), sds((2 * slabs * 8, 128), BF16), sds((4 * blocks * 8, slabs * 8), BF16)),
         [pltpu.VMEM(noisy.shape, F32)],
         10**6,
         10**6,
         8,
     )
     recv = lax.all_to_all(send, "tensor", split_axis=0, concat_axis=0, tiled=True)
-    routed = clean_call(rows, peers, slabs, feats, recv, side)
+    routed = clean_call(peers, slabs, feats, recv, side, route)
     landed = lax.all_to_all(routed, "wide", split_axis=0, concat_axis=0, tiled=True)
-    copies = pick_call(rows, peers, slabs, here, landed)
+    copies = pick_call(peers, choose, landed)
     latents = lax.all_to_all(copies, "tensor", split_axis=0, concat_axis=0, tiled=True)
     own = lax.dynamic_slice_in_dim(conv1_weight, t * outs, outs, 2)
     w1 = own.transpose(0, 2, 1).reshape(9 * outs, -1)

time: 82.1 us -> 81.7 us (level)
  no operation moved by 1% of the time
where the time goes in v4:
time: 81.7 us; the launch traced here: 81.3 us
  blocking collectives  38 us (47%)
  Pallas kernels  14.2 us (17%)
  waiting for transfers between devices  12.4 us (15%)
  starting transfers between devices  11.7 us (14%)
  local copies, waits for them, and re-layouts  2.89 us (4%)
  between operations  1.34 us (2%)
    all_to_all x1, blocking collectives, shards(): lax.all_to_all(routed, 'wide', split_axis=0, concat_axis=0, tiled=True)  38 us
    pallas_call x6, Pallas kernels, call(): pl.pallas_call(body, out_shape=out_shape, in_specs=[pl.BlockSpec(memory_s...  14.2 us
    all_to_all x1, starting transfers between devices, shards(): lax.all_to_all(send, 'tensor', split_axis=0, concat_axis=0, tiled=True)  8 us
    all_to_all x1, waiting for transfers between devices, shards(): lax.all_to_all(send, 'tensor', split_axis=0, concat_axis=0, tiled=True)  7.39 us
    all_to_all x1, waiting for transfers between devices, shards(): lax.all_to_all(copies, 'tensor', split_axis=0, concat_axis=0, tiled=True)  5.02 us
    all_to_all x1, starting transfers between devices, shards(): lax.all_to_all(copies, 'tensor', split_axis=0, concat_axis=0, tiled=True)  3.7 us
    transpose x2, local copies, waits for them, and re-layouts, shards(): w1 = own.transpose(0, 2, 1).reshape(9 * outs, -1)  2.05 us
  transfers between devices with their start and end apart: 2, of which 2 were waited for; matrix products, arithmetic and copies ran while one was open for 4% of the time, Pallas kernels for 3%

profile of v4, /device:TPU:1, one launch (start us, length us, event | category | flops | bytes accessed | tf_op | source)
XLA Modules:
  0.0 81.3 jit_solution(14290946885351313753)
XLA Ops:
  0.6 0.0 copy-start
  0.6 3.0 %shard_map.114 = bf16[1536,128]{1,0:T(8,128)(2,1)} custom-call(bf16[192,1536]{1,0:T(8,128)(2,1)} %bitcast.24, f32[2,192]{1,0:T(2,128)} %rest_0_.1, bf16[64,192]{1,0:T(8,128)(2,1)} %bitcast.25, bf16[32,144]{1,0:T(8,128)(2,1)} %bitcast.26, f32[1,32]{1,0:T(1,128)} %bitcast.27), custom_call_target="tpu_custom_call" | custom-call | flops 1000000000 | bytes 2000000 | tf_op jit(solution)/shard_map/pallas_call | solution.py:332
  3.6 8.0 %all-to-all-start = ((bf16[16,96,128]{2,1,0:T(8,128)(2,1)}), bf16[16,96,128]{2,1,0:T(8,128)(2,1)S(1)}, u32[]{:S(2)}, u32[]{:S(2)}) async-start(bf16[16,96,128]{2,1,0:T(8,128)(2,1)} %bitcast.23), calls=%async_computation | async-start | bytes 786432 | tf_op jit(solution)/shard_map/all_to_all | solution.py:456
  12.3 0.7 pad_add_fusion.here
  13.0 0.0 copy-done
  13.0 1.2 %shard_map.113 = (f32[56,128]{1,0:T(8,128)S(1)}, bf16[768,128]{1,0:T(8,128)(2,1)S(1)}, bf16[224,384]{1,0:T(8,128)(2,1)S(1)}) custom-call(s32[27]{0:T(128)S(1)} %pad_add_fusion.here, f32[64,1536]{1,0:T(8,128)S(1)} %bitcast.18), custom_call_target="tpu_custom_call" | custom-call | flops 1000000 | bytes 1000000 | tf_op jit(solution)/shard_map/pallas_call | solution.py:332
  14.2 7.4 %all-to-all-done = bf16[16,96,128]{2,1,0:T(8,128)(2,1)S(1)} async-done(((bf16[16,96,128]{2,1,0:T(8,128)(2,1)}), bf16[16,96,128]{2,1,0:T(8,128)(2,1)S(1)}, u32[]{:S(2)}, u32[]{:S(2)}) %all-to-all-start) | async-done | bytes 393248 | tf_op jit(solution)/shard_map/all_to_all | solution.py:456
  21.6 1.0 %shard_map.115 = bf16[384,128]{1,0:T(8,128)(2,1)S(1)} custom-call(bf16[1536,128]{1,0:T(8,128)(2,1)S(1)} %bitcast.16, f32[56,128]{1,0:T(8,128)S(1)} %get-tuple-element.8.side_ref, bf16[768,128]{1,0:T(8,128)(2,1)S(1)} %get-tuple-element.9.route_ref), custom_call_target="tpu_custom_call" | custom-call | flops 10000000 | bytes 1000000 | tf_op jit(solution)/shard_map/pallas_call | solution.py:332
  22.6 38.0 %all_to_all.33 = bf16[48,8,128]{2,1,0:T(8,128)(2,1)S(1)} all-to-all(bf16[48,8,128]{2,1,0:T(8,128)(2,1)S(1)} %bitcast.20), channel_id=1, replica_groups=mesh['wide'=48,'tensor'=16] {'wide'}, dimensions={0} | all-to-all | bytes 196608 | tf_op jit(solution)/shard_map/all_to_all | solution.py:458
  60.7 1.0 %shard_map.116 = bf16[128,896]{1,0:T(8,128)(2,1)} custom-call(bf16[224,384]{1,0:T(8,128)(2,1)S(1)} %get-tuple-element.7.choose_ref, bf16[384,128]{1,0:T(8,128)(2,1)S(1)} %bitcast.19), custom_call_target="tpu_custom_call" | custom-call | flops 10000000 | bytes 1000000 | tf_op jit(solution)/shard_map/pallas_call | solution.py:332
  61.6 3.7 %all-to-all-start.2 = ((bf16[16,8,896]{2,1,0:T(8,128)(2,1)}), bf16[16,8,896]{2,1,0:T(8,128)(2,1)S(1)}, u32[]{:S(2)}, u32[]{:S(2)}) async-start(bf16[16,8,896]{2,1,0:T(8,128)(2,1)} %bitcast.11), calls=%async_computation.2 | async-start | bytes 458752 | tf_op jit(solution)/shard_map/all_to_all | solution.py:460
  65.3 1.7 %dynamic-slice_bitcast_fusion = bf16[9,32,512]{1,2,0:T(8,128)(2,1)S(1)} fusion(bf16[9,512,512]{2,1,0:T(8,128)(2,1)} %param.18, s32[]{:T(128)S(6)} %select_n.4), kind=kLoop, calls=%fused_computation | loop fusion | bytes 589828 | tf_op jit(solution)/shard_map/transpose | solution.py:462
  67.0 0.4 copy.12
  67.4 0.8 dynamic_slice.7
  68.2 1.5 %shard_map.117 = (bf16[544,144]{1,0:T(8,128)(2,1)S(1)}, f32[544,128]{1,0:T(8,128)S(1)}) custom-call(s32[27]{0:T(128)S(1)} %pad_add_fusion.here, bf16[1536,128]{1,0:T(8,128)(2,1)S(1)} %bitcast.17), custom_call_target="tpu_custom_call" | custom-call | flops 1000000 | bytes 1000000 | tf_op jit(solution)/shard_map/pallas_call | solution.py:332
  69.6 5.0 %all-to-all-done.2 = bf16[16,8,896]{2,1,0:T(8,128)(2,1)S(1)} async-done(((bf16[16,8,896]{2,1,0:T(8,128)(2,1)}), bf16[16,8,896]{2,1,0:T(8,128)(2,1)S(1)}, u32[]{:S(2)}, u32[]{:S(2)}) %all-to-all-start.2) | async-done | bytes 229408 | tf_op jit(solution)/shard_map/all_to_all | solution.py:460
  74.6 0.1 broadcast_in_dim.2.b1_ref
  74.7 6.6 %shard_map.118 = (bf16[48,32,128]{2,1,0:T(8,128)(2,1)}, bf16[48,32,128]{2,1,0:T(8,128)(2,1)}) custom-call(s32[27]{0:T(128)S(1)} %pad_add_fusion.here, bf16[128,896]{1,0:T(8,128)(2,1)S(1)} %bitcast.22, bf16[544,144]{1,0:T(8,128)(2,1)S(1)} %get-tuple-element.10.weight, f32[544,128]{1,0:T(8,128)S(1)} %get-tuple-element.11.bias, bf16[288,512]{1,0:T(8,128)(2,1)S(1)} %bitcast.21, ...), custom_call_target="tpu_custom_call" | custom-call | flops 6000000000 | bytes 3000000 | tf_op jit(solution)/shard_map/pallas_call | solution.py:332
Async XLA Ops:
  0.6 12.4 %copy-start = (f32[1536,64]{0,1:T(8,128)S(1)}, f32[1536,64]{0,1:T(8,128)}, u32[]{:S(2)}) copy-start(f32[1536,64]{0,1:T(8,128)} %param.13) | copy-start | bytes 1179652
  3.6 18.0 %all-to-all-start = ((bf16[16,96,128]{2,1,0:T(8,128)(2,1)}), bf16[16,96,128]{2,1,0:T(8,128)(2,1)S(1)}, u32[]{:S(2)}, u32[]{:S(2)}) async-start(bf16[16,96,128]{2,1,0:T(8,128)(2,1)} %bitcast.23), calls=%async_computation | async-start | bytes 786432 | tf_op jit(solution)/shard_map/all_to_all | solution.py:456
  61.6 13.0 %all-to-all-start.2 = ((bf16[16,8,896]{2,1,0:T(8,128)(2,1)}), bf16[16,8,896]{2,1,0:T(8,128)(2,1)S(1)}, u32[]{:S(2)}, u32[]{:S(2)}) async-start(bf16[16,8,896]{2,1,0:T(8,128)(2,1)} %bitcast.11), calls=%async_computation.2 | async-start | bytes 458752 | tf_op jit(solution)/shard_map/all_to_all | solution.py:460

commit v5 on v4

--- a/solution.py
+++ b/solution.py
@@ -20,8 +20,9 @@
 
 SR = 24
 STAT = 2 * SR
-WROW = STAT + 16
-BLOCK = WROW + 32
+BLOCK = STAT + 16
+WBLOCK = 48
+STEPS_AWAY = (8, 4, 2, 1)
 
 
 def iota(shape, dim):
@@ -47,7 +48,7 @@
 
 def project_kernel(rows, peers, h_hbm, *rest):
     small = rest[:4]
-    send_ref, h_ref, mod_ref, w_ref, win_ref, bin_ref, sums, sems = rest[4:]
+    send_ref, weight_ref, h_ref, mod_ref, w_ref, win_ref, bin_ref, sums, sems = rest[4:]
     moves = list(zip(small, (mod_ref, w_ref, win_ref, bin_ref)))
     moves.append((h_hbm, h_ref))
     copies = [pltpu.make_async_copy(src, dst, sems.at[n]) for n, (src, dst) in enumerate(moves)]
@@ -83,11 +84,12 @@
     pad = jnp.zeros((1, 64), F32)
     lines = thirds(to_row(colsum)) + thirds(to_row(shifted))
     lower = jnp.concatenate([jnp.concatenate([v, pad], axis=1) for v in lines] + [jnp.zeros((2, 128), F32)], axis=0)
-    upper = jnp.zeros((8, 128), F32)
+    ends = jnp.zeros((8, 128), F32)
     for g in range(outs // 8):
-        upper = upper + pltpu.roll(bias[8 * g : 8 * g + 8, :], 72 + 4 * g, 1)
-        lower = lower + pltpu.roll(rest_w[8 * g : 8 * g + 8, :], 64 + 16 * g, 1)
-    main_w = win_ref[:, :128]
+        ends = ends + pltpu.roll(bias[8 * g : 8 * g + 8, :], 64 + 4 * g, 1)
+        ends = ends + (pltpu.roll(rest_w[8 * g : 8 * g + 8, :], 16 * g, 1) if g else rest_w[:8, :])
+    held = jnp.concatenate([win[:, :128], ends, jnp.zeros((WBLOCK - outs - 8, 128), F32)], axis=0).astype(BF16)
+    weight_ref[...] = held
     fill = [jnp.zeros((SR - rows, 128), F32)] if rows < SR else []
     for peer in range(peers):
         base = peer * BLOCK
@@ -102,11 +104,10 @@
         for half in range(per // 2):
             joined = jnp.where(low, halves[2 * half], halves[2 * half + 1])
             send_ref[base + half * SR : base + (half + 1) * SR, :] = joined.astype(BF16)
-        tile = upper
-        for g in range(SR // 8):
-            tile = tile + (pltpu.roll(stat[8 * g : 8 * g + 8, :], 24 * g, 1) if g else stat[:8, :])
+        tile = stat[:8, :]
+        for g in range(1, SR // 8):
+            tile = tile + pltpu.roll(stat[8 * g : 8 * g + 8, :], 24 * g, 1)
         send_ref[base + STAT : base + STAT + 16, :] = jnp.concatenate([tile, lower], axis=0).astype(BF16)
-        send_ref[base + WROW : base + WROW + 32, :] = main_w
 
 
 def side_kernel(rows, peers, slabs, here, noisy_ref, side_ref, route_ref, choose_ref, drawn):
@@ -234,18 +235,21 @@
     outs = weight.shape[0] // (peers + 1)
 
     def load(base, at):
-        tile = recv_ref[pl.ds(pl.multiple_of(base + STAT, 16), 16), :].astype(F32)
+        block = recv_ref[base : base + WBLOCK, :]
+        tile = block[outs : outs + 8, :].astype(F32)
         groups = range(outs // 8)
-        side = jnp.concatenate([pltpu.roll(tile[8:, :], 64 - 16 * g, 1) for g in groups], axis=0)
-        turned = jnp.concatenate([pltpu.roll(tile[:8, :], 56 - 4 * g, 1) for g in groups], axis=0)
-        weight[at : at + outs, :128] = recv_ref[pl.ds(pl.multiple_of(base + WROW, 16), 32), :]
-        weight[at : at + outs, 128:] = side[:, :16].astype(BF16)
+        side = jnp.concatenate([pltpu.roll(tile, 128 - 16 * g, 1) if g else tile for g in groups], axis=0)
+        turned = jnp.concatenate([pltpu.roll(tile, 64 - 4 * g, 1) for g in groups], axis=0)
+        at = pl.ds(pl.multiple_of(at * outs, outs), outs)
+        weight[at, :128] = block[:outs, :]
+        weight[at, 128:] = side[:, :16].astype(BF16)
         total = turned[:, 0:1] + turned[:, 1:2] + turned[:, 2:3]
-        bias[at : at + outs, :] = jnp.broadcast_to(total, (outs, 128))
-
-    for peer in range(peers):
-        load(peer * BLOCK, peer * outs)
-    load(here[0] * BLOCK, peers * outs)
+        bias[at, :] = jnp.broadcast_to(total, (outs, 128))
+
+    for slot in range(peers):
+        away = sum(bit for n, bit in enumerate(STEPS_AWAY) if slot >> n & 1)
+        load(slot * WBLOCK, jnp.bitwise_xor(here[0], away))
+    load(0, peers)
 
 
 def decode_kernel(rows, here, lat_ref, weight, bias, w1_ref, b1_ref, dec_ref, res_ref, spread_out, shifted, act, act2, tap0, tap1, tap2, tap3):
@@ -278,7 +282,7 @@
         for n in range(2):
             q = 2 * m + n
             global_row = lax.rem(first_row - 1 + q + WPIX, WPIX)
-            block = shifted[q * 48 : q * 48 + 144, :]
+            block = shifted[pl.ds(pl.multiple_of(q * 48, 16), 144), :]
             up = jnp.where(global_row != 0, block[:48, :], jnp.zeros((48, 128), BF16))
             down = jnp.where(global_row != WPIX - 1, block[96:, :], jnp.zeros((48, 128), BF16))
             parts.append(jnp.concatenate([up, block[48:96, :], down], axis=0))
@@ -286,10 +290,8 @@
         feat = jnp.dot(weight[...], right, preferred_element_type=F32)
         both = jnp.concatenate([bias[...], bias[...]], axis=1)
         feat = (feat + both).astype(BF16)
-        if m > 0:
-            dec_ref[2 * m - 1] = feat[all_out:, :128]
-        if m < rows:
-            dec_ref[2 * m] = feat[all_out:, 128:]
+        dec_ref[jnp.minimum(2 * m, slab_height - 1)] = feat[all_out:, 128:]
+        dec_ref[jnp.abs(2 * m - 1)] = feat[all_out:, :128]
         value = feat[:all_out, :].astype(F32)
         halved = 0.5 * value
         buf[...] = (halved + halved * jnp.tanh(halved)).astype(BF16)
@@ -313,13 +315,20 @@
             res_ref[y] = total.astype(BF16)
 
     acts = (act, act2)
+    features(0, act)
+    tap2[...] = jnp.zeros_like(tap2)
+    tap3[...] = jnp.zeros_like(tap3)
     taps = (tap0, tap1, tap2, tap3)
-    features(0, act)
-    for m in range(1, rows + 1):
-        if m > 2:
-            finish(m - 2, taps[(m + 1) % 4], taps[(m + 2) % 4])
-        features(m, acts[m % 2])
-        multiply(m - 1, acts[(m - 1) % 2], taps[(m - 1) % 4])
+
+    def several(step, carry):
+        for n in range(12):
+            m = 12 * step + 1 + n
+            finish(jnp.maximum(m - 2, 1), taps[(n + 2) % 4], taps[(n + 3) % 4])
+            features(m, acts[(n + 1) % 2])
+            multiply(m - 1, acts[n % 2], taps[n % 4])
+        return carry
+
+    lax.fori_loop(0, rows // 12, several, 0)
     finish(rows - 1, taps[(rows - 2) % 4], taps[(rows - 1) % 4])
     multiply(rows, acts[rows % 2], taps[rows % 4])
     finish(rows, taps[(rows - 1) % 4], taps[rows % 4])
@@ -384,7 +393,7 @@
         functools.partial(project_kernel, rows, peers),
         large,
         "hhhhh",
-        jax.ShapeDtypeStruct((peers * BLOCK, 128), BF16),
+        (jax.ShapeDtypeStruct((peers * BLOCK, 128), BF16), jax.ShapeDtypeStruct((WBLOCK, 128), BF16)),
         [pltpu.VMEM(x.shape, x.dtype) for x in large]
         + [pltpu.VMEM((hidden.shape[1], 128), F32), pltpu.SemaphoreType.DMA((5,))],
         10**9,
@@ -441,7 +450,7 @@
     outs = conv_in_weight.shape[1]
     sds = jax.ShapeDtypeStruct
     small = (modulation, final_weight.T, conv_in_weight.T, conv_in_bias.reshape(1, -1))
-    send = project_call(rows, peers, hidden.T, small)
+    send, shard = project_call(rows, peers, hidden.T, small)
     blocks = ((rows + 2) // 2 + 1) // 2
     side, route, choose = call(
         functools.partial(side_kernel, rows, peers, slabs),
@@ -455,13 +464,17 @@
     )
     recv = lax.all_to_all(send, "tensor", split_axis=0, concat_axis=0, tiled=True)
     routed = clean_call(peers, slabs, feats, recv, side, route)
+
     landed = lax.all_to_all(routed, "wide", split_axis=0, concat_axis=0, tiled=True)
+    for bit in STEPS_AWAY:
+        pairs = [(i, i ^ bit) for i in range(peers)]
+        shard = jnp.concatenate([shard, lax.ppermute(shard, "tensor", pairs)], axis=0)
     copies = pick_call(peers, choose, landed)
     latents = lax.all_to_all(copies, "tensor", split_axis=0, concat_axis=0, tiled=True)
     own = lax.dynamic_slice_in_dim(conv1_weight, t * outs, outs, 2)
     w1 = own.transpose(0, 2, 1).reshape(9 * outs, -1)
     b1 = jnp.broadcast_to(lax.dynamic_slice_in_dim(conv1_bias, t * outs, outs, 0)[:, None], (outs, 128))
-    weight, bias = gather_call(here, recv, peers, outs)
+    weight, bias = gather_call(here, shard, peers, outs)
     return decode_call(rows, here, latents, weight, bias, w1, b1)
 
 

time: 81.7 us -> 81 us (level)
  blocking collectives: 38 us -> 0 us
  starting transfers between devices: 11.7 us -> 46 us
  waiting for transfers between devices: 12.4 us -> 14.6 us
    all_to_all x1 -> x0, blocking collectives: 38 us -> none  [shards(): lax.all_to_all(routed, 'wide', split_axis=0, concat_axis=0, tiled=True)]
    all_to_all x0 -> x1, starting transfers between devices: none -> 20.3 us  [shards(): lax.all_to_all(routed, 'wide', split_axis=0, concat_axis=0, tiled=True)]
    ppermute x0 -> x4, starting transfers between devices: none -> 13.5 us  [shards(): lax.ppermute(shard, 'tensor', pairs)]
    all_to_all x1, waiting for transfers between devices: 7.39 us -> 0.01 us  [shards(): lax.all_to_all(send, 'tensor', split_axis=0, concat_axis=0, tiled=True)]
    all_to_all x0 -> x1, waiting for transfers between devices: none -> 7.22 us  [shards(): lax.all_to_all(routed, 'wide', split_axis=0, concat_axis=0, tiled=True)]
    ppermute x0 -> x4, waiting for transfers between devices: none -> 6.47 us  [shards(): lax.ppermute(shard, 'tensor', pairs)]
    all_to_all x1, waiting for transfers between devices: 5.02 us -> 0.88 us  [shards(): lax.all_to_all(copies, 'tensor', split_axis=0, concat_axis=0, tiled=True)]
  transfers between devices with their start and end apart: 2 -> 7, of which waited for: 2 -> 4; matrix products, arithmetic and copies ran while one was open for 4% -> 5% of each run, Pallas kernels for 3% -> 6%
where the time goes in v5:
time: 81 us; the launch traced here: 80.3 us
  starting transfers between devices  46 us (57%)
  waiting for transfers between devices  14.6 us (18%)
  Pallas kernels  14.5 us (18%)
  local copies, waits for them, and re-layouts  3.64 us (4%)
  between operations  1.47 us (2%)
    all_to_all x1, starting transfers between devices, shards(): lax.all_to_all(routed, 'wide', split_axis=0, concat_axis=0, tiled=True)  20.3 us
    pallas_call x6, Pallas kernels, call(): pl.pallas_call(body, out_shape=out_shape, in_specs=[pl.BlockSpec(memory_s...  14.5 us
    ppermute x4, starting transfers between devices, shards(): lax.ppermute(shard, 'tensor', pairs)  13.5 us
    all_to_all x1, starting transfers between devices, shards(): lax.all_to_all(send, 'tensor', split_axis=0, concat_axis=0, tiled=True)  8 us
    all_to_all x1, waiting for transfers between devices, shards(): lax.all_to_all(routed, 'wide', split_axis=0, concat_axis=0, tiled=True)  7.22 us
    ppermute x4, waiting for transfers between devices, shards(): lax.ppermute(shard, 'tensor', pairs)  6.47 us
    all_to_all x1, starting transfers between devices, shards(): lax.all_to_all(copies, 'tensor', split_axis=0, concat_axis=0, tiled=True)  4.26 us
    transpose x2, local copies, waits for them, and re-layouts, shards(): w1 = own.transpose(0, 2, 1).reshape(9 * outs, -1)  2.04 us
  transfers between devices with their start and end apart: 7, of which 4 were waited for; matrix products, arithmetic and copies ran while one was open for 5% of the time, Pallas kernels for 6%

profile of v5, /device:TPU:1, one launch (start us, length us, event | category | flops | bytes accessed | tf_op | source)
XLA Modules:
  0.0 80.3 jit_solution(2244275596111339143)
XLA Ops:
  0.6 0.0 copy-start.2
  0.6 0.0 copy-start
  0.7 2.9 %shard_map.114 = (bf16[1024,128]{1,0:T(8,128)(2,1)}, bf16[48,128]{1,0:T(8,128)(2,1)}) custom-call(bf16[192,1536]{1,0:T(8,128)(2,1)} %bitcast.22, f32[2,192]{1,0:T(2,128)} %rest_0_.1, bf16[64,192]{1,0:T(8,128)(2,1)} %bitcast.23, bf16[32,144]{1,0:T(8,128)(2,1)} %bitcast.24, f32[1,32]{1,0:T(1,128)} %bitcast.25), custom_call_target="tpu_custom_call" | custom-call | flops 1000000000 | bytes 2000000 | tf_op jit(solution)/shard_map/pallas_call | solution.py:341
  3.6 0.0 copy-start.1
  3.6 8.0 %all-to-all-start = ((bf16[16,64,128]{2,1,0:T(8,128)(2,1)}), bf16[16,64,128]{2,1,0:T(8,128)(2,1)S(1)}, u32[]{:S(2)}, u32[]{:S(2)}) async-start(bf16[16,64,128]{2,1,0:T(8,128)(2,1)} %bitcast.21), calls=%async_computation | async-start | bytes 524288 | tf_op jit(solution)/shard_map/all_to_all | solution.py:465
  11.6 4.2 %collective-permute-start = (bf16[48,128]{1,0:T(8,128)(2,1)}, bf16[48,128]{1,0:T(8,128)(2,1)S(1)}, u32[]{:S(2)}, u32[]{:S(2)}) collective-permute-start(bf16[48,128]{1,0:T(8,128)(2,1)} %get-tuple-element.13), channel_id=1, source_target_pairs={{0,8},{1,9},{2,10},{3,11},{4,12},{5,13},{6,14},{7,15},{8,0},{9,1},... | collective-permute-start | bytes 36872 | tf_op jit(solution)/shard_map/ppermute | solution.py:471
  16.4 0.7 constant_dynamic-update-slice_fusion.4
  17.2 1.7 %dynamic-slice_bitcast_fusion = bf16[9,32,512]{1,2,0:T(8,128)(2,1)S(1)} fusion(bf16[9,512,512]{2,1,0:T(8,128)(2,1)} %param.18, s32[]{:T(128)S(6)} %select_n.4), kind=kLoop, calls=%fused_computation | loop fusion | bytes 589828 | tf_op jit(solution)/shard_map/transpose | solution.py:475
  18.8 0.0 copy-done.2
  18.8 0.1 pad_add_fusion.here
  18.9 0.4 copy.12
  19.3 0.8 dynamic_slice.7
  20.1 0.0 copy-done
  20.1 1.2 %shard_map.113 = (f32[56,128]{1,0:T(8,128)S(1)}, bf16[768,128]{1,0:T(8,128)(2,1)S(1)}, bf16[224,384]{1,0:T(8,128)(2,1)S(1)}) custom-call(s32[27]{0:T(128)S(1)} %pad_add_fusion.here, f32[64,1536]{1,0:T(8,128)S(1)} %bitcast.17), custom_call_target="tpu_custom_call" | custom-call | flops 1000000 | bytes 1000000 | tf_op jit(solution)/shard_map/pallas_call | solution.py:341
  21.3 0.0 all-to-all-done
  21.3 1.6 %shard_map.115 = bf16[384,128]{1,0:T(8,128)(2,1)} custom-call(bf16[1024,128]{1,0:T(8,128)(2,1)S(1)} %bitcast.16, f32[56,128]{1,0:T(8,128)S(1)} %get-tuple-element.11.side_ref, bf16[768,128]{1,0:T(8,128)(2,1)S(1)} %get-tuple-element.12.route_ref), custom_call_target="tpu_custom_call" | custom-call | flops 10000000 | bytes 1000000 | tf_op jit(solution)/shard_map/pallas_call | solution.py:341
  22.9 20.3 %all-to-all-start.1 = ((bf16[48,8,128]{2,1,0:T(8,128)(2,1)}), bf16[48,8,128]{2,1,0:T(8,128)(2,1)S(1)}, u32[]{:S(2)}, u32[]{:S(2)}) async-start(bf16[48,8,128]{2,1,0:T(8,128)(2,1)} %bitcast.9), calls=%async_computation.1 | async-start | bytes 196608 | tf_op jit(solution)/shard_map/all_to_all | solution.py:468
  43.2 0.0 collective-permute-done
  43.2 0.0 copy-done.1
  43.2 2.4 %collective-permute-start.1 = (bf16[96,128]{1,0:T(8,128)(2,1)S(1)}, bf16[96,128]{1,0:T(8,128)(2,1)S(1)}, u32[]{:S(2)}, u32[]{:S(2)}) collective-permute-start(bf16[96,128]{1,0:T(8,128)(2,1)S(1)} %pad_maximum_fusion.2), channel_id=1, source_target_pairs={{0,4},{1,5},{2,6},{3,7},{4,0},{5,1},{6,2},{7,3},{8,12},{9,13},{10,... | collective-permute-start | bytes 73736 | tf_op jit(solution)/shard_map/ppermute | solution.py:471
  45.6 2.7 %collective-permute-done.1 = bf16[96,128]{1,0:T(8,128)(2,1)S(1)} collective-permute-done((bf16[96,128]{1,0:T(8,128)(2,1)S(1)}, bf16[96,128]{1,0:T(8,128)(2,1)S(1)}, u32[]{:S(2)}, u32[]{:S(2)}) %collective-permute-start.1) | collective-permute-done | bytes 24608 | tf_op jit(solution)/shard_map/ppermute | solution.py:471
  48.3 3.7 %collective-permute-start.2 = (bf16[192,128]{1,0:T(8,128)(2,1)S(1)}, bf16[192,128]{1,0:T(8,128)(2,1)S(1)}, u32[]{:S(2)}, u32[]{:S(2)}) collective-permute-start(bf16[192,128]{1,0:T(8,128)(2,1)S(1)} %pad_maximum_fusion.1), channel_id=1, source_target_pairs={{0,2},{1,3},{2,0},{3,1},{4,6},{5,7},{6,4},{7,5},{8,10},{9,11},{10,... | collective-permute-start | bytes 147464 | tf_op jit(solution)/shard_map/ppermute | solution.py:471
  52.0 7.2 %all-to-all-done.1 = bf16[48,8,128]{2,1,0:T(8,128)(2,1)S(1)} async-done(((bf16[48,8,128]{2,1,0:T(8,128)(2,1)}), bf16[48,8,128]{2,1,0:T(8,128)(2,1)S(1)}, u32[]{:S(2)}, u32[]{:S(2)}) %all-to-all-start.1) | async-done | bytes 98336 | tf_op jit(solution)/shard_map/all_to_all | solution.py:468
  59.2 1.0 %shard_map.116 = bf16[128,896]{1,0:T(8,128)(2,1)} custom-call(bf16[224,384]{1,0:T(8,128)(2,1)S(1)} %get-tuple-element.9.choose_ref, bf16[384,128]{1,0:T(8,128)(2,1)S(1)} %bitcast.18), custom_call_target="tpu_custom_call" | custom-call | flops 10000000 | bytes 1000000 | tf_op jit(solution)/shard_map/pallas_call | solution.py:341
  60.2 4.3 %all-to-all-start.2 = ((bf16[16,8,896]{2,1,0:T(8,128)(2,1)}), bf16[16,8,896]{2,1,0:T(8,128)(2,1)S(1)}, u32[]{:S(2)}, u32[]{:S(2)}) async-start(bf16[16,8,896]{2,1,0:T(8,128)(2,1)} %bitcast.11), calls=%async_computation.2 | async-start | bytes 458752 | tf_op jit(solution)/shard_map/all_to_all | solution.py:473
  64.5 0.0 collective-permute-done.2
  64.5 3.3 %collective-permute-start.3 = (bf16[384,128]{1,0:T(8,128)(2,1)S(1)}, bf16[384,128]{1,0:T(8,128)(2,1)S(1)}, u32[]{:S(2)}, u32[]{:S(2)}) collective-permute-start(bf16[384,128]{1,0:T(8,128)(2,1)S(1)} %pad_maximum_fusion), channel_id=1, source_target_pairs={{0,1},{1,0},{2,3},{3,2},{4,5},{5,4},{6,7},{7,6},{8,9},{9,8},{10,11... | collective-permute-start | bytes 294920 | tf_op jit(solution)/shard_map/ppermute | solution.py:471
  67.8 3.8 %collective-permute-done.3 = bf16[384,128]{1,0:T(8,128)(2,1)S(1)} collective-permute-done((bf16[384,128]{1,0:T(8,128)(2,1)S(1)}, bf16[384,128]{1,0:T(8,128)(2,1)S(1)}, u32[]{:S(2)}, u32[]{:S(2)}) %collective-permute-start.3) | collective-permute-done | bytes 98336 | tf_op jit(solution)/shard_map/ppermute | solution.py:471
  71.6 1.3 %shard_map.117 = (bf16[544,144]{1,0:T(8,128)(2,1)S(1)}, f32[544,128]{1,0:T(8,128)S(1)}) custom-call(s32[27]{0:T(128)S(1)} %pad_add_fusion.here, bf16[768,128]{1,0:T(8,128)(2,1)S(1)} %constant_dynamic-update-slice_fusion.recv_ref), custom_call_target="tpu_custom_call" | custom-call | flops 1000000 | bytes 1000000 | tf_op jit(solution)/shard_map/pallas_call | solution.py:341
  72.9 0.9 %all-to-all-done.2 = bf16[16,8,896]{2,1,0:T(8,128)(2,1)S(1)} async-done(((bf16[16,8,896]{2,1,0:T(8,128)(2,1)}), bf16[16,8,896]{2,1,0:T(8,128)(2,1)S(1)}, u32[]{:S(2)}, u32[]{:S(2)}) %all-to-all-start.2) | async-done | bytes 229408 | tf_op jit(solution)/shard_map/all_to_all | solution.py:473
  73.8 0.1 broadcast_in_dim.2.b1_ref
  73.8 6.5 %shard_map.118 = (bf16[48,32,128]{2,1,0:T(8,128)(2,1)}, bf16[48,32,128]{2,1,0:T(8,128)(2,1)}) custom-call(s32[27]{0:T(128)S(1)} %pad_add_fusion.here, bf16[128,896]{1,0:T(8,128)(2,1)S(1)} %bitcast.20, bf16[544,144]{1,0:T(8,128)(2,1)S(1)} %get-tuple-element.14.weight, f32[544,128]{1,0:T(8,128)S(1)} %get-tuple-element.15.bias, bf16[288,512]{1,0:T(8,128)(2,1)S(1)} %bitcast.19, ...), custom_call_target="tpu_custom_call" | custom-call | flops 6000000000 | bytes 3000000 | tf_op jit(solution)/shard_map/pallas_call | solution.py:341
  (7 shorter events, 0.1 us)
Async XLA Ops:
  0.6 18.2 %copy-start.2 = (s32[24]{0:T(128)S(1)}, s32[24]{0:T(128)}, u32[]{:S(2)}) copy-start(s32[24]{0:T(128)} %param.15) | copy-start | bytes 292
  0.6 19.4 %copy-start = (f32[1536,64]{0,1:T(8,128)S(1)}, f32[1536,64]{0,1:T(8,128)}, u32[]{:S(2)}) copy-start(f32[1536,64]{0,1:T(8,128)} %param.13) | copy-start | bytes 1179652
  3.6 39.6 %copy-start.1 = (bf16[48,128]{1,0:T(8,128)(2,1)S(1)}, bf16[48,128]{1,0:T(8,128)(2,1)}, u32[]{:S(2)}) copy-start(bf16[48,128]{1,0:T(8,128)(2,1)} %get-tuple-element.13) | copy-start | bytes 36868
  3.6 17.7 %all-to-all-start = ((bf16[16,64,128]{2,1,0:T(8,128)(2,1)}), bf16[16,64,128]{2,1,0:T(8,128)(2,1)S(1)}, u32[]{:S(2)}, u32[]{:S(2)}) async-start(bf16[16,64,128]{2,1,0:T(8,128)(2,1)} %bitcast.21), calls=%async_computation | async-start | bytes 524288 | tf_op jit(solution)/shard_map/all_to_all | solution.py:465
  11.6 31.6 %collective-permute-start = (bf16[48,128]{1,0:T(8,128)(2,1)}, bf16[48,128]{1,0:T(8,128)(2,1)S(1)}, u32[]{:S(2)}, u32[]{:S(2)}) collective-permute-start(bf16[48,128]{1,0:T(8,128)(2,1)} %get-tuple-element.13), channel_id=1, source_target_pairs={{0,8},{1,9},{2,10},{3,11},{4,12},{5,13},{6,14},{7,15},{8,0},{9,1},... | collective-permute-start | bytes 36872 | tf_op jit(solution)/shard_map/ppermute | solution.py:471
  22.9 36.3 %all-to-all-start.1 = ((bf16[48,8,128]{2,1,0:T(8,128)(2,1)}), bf16[48,8,128]{2,1,0:T(8,128)(2,1)S(1)}, u32[]{:S(2)}, u32[]{:S(2)}) async-start(bf16[48,8,128]{2,1,0:T(8,128)(2,1)} %bitcast.9), calls=%async_computation.1 | async-start | bytes 196608 | tf_op jit(solution)/shard_map/all_to_all | solution.py:468
  43.2 5.1 %collective-permute-start.1 = (bf16[96,128]{1,0:T(8,128)(2,1)S(1)}, bf16[96,128]{1,0:T(8,128)(2,1)S(1)}, u32[]{:S(2)}, u32[]{:S(2)}) collective-permute-start(bf16[96,128]{1,0:T(8,128)(2,1)S(1)} %pad_maximum_fusion.2), channel_id=1, source_target_pairs={{0,4},{1,5},{2,6},{3,7},{4,0},{5,1},{6,2},{7,3},{8,12},{9,13},{10,... | collective-permute-start | bytes 73736 | tf_op jit(solution)/shard_map/ppermute | solution.py:471
  48.3 16.2 %collective-permute-start.2 = (bf16[192,128]{1,0:T(8,128)(2,1)S(1)}, bf16[192,128]{1,0:T(8,128)(2,1)S(1)}, u32[]{:S(2)}, u32[]{:S(2)}) collective-permute-start(bf16[192,128]{1,0:T(8,128)(2,1)S(1)} %pad_maximum_fusion.1), channel_id=1, source_target_pairs={{0,2},{1,3},{2,0},{3,1},{4,6},{5,7},{6,4},{7,5},{8,10},{9,11},{10,... | collective-permute-start | bytes 147464 | tf_op jit(solution)/shard_map/ppermute | solution.py:471
  60.2 13.6 %all-to-all-start.2 = ((bf16[16,8,896]{2,1,0:T(8,128)(2,1)}), bf16[16,8,896]{2,1,0:T(8,128)(2,1)S(1)}, u32[]{:S(2)}, u32[]{:S(2)}) async-start(bf16[16,8,896]{2,1,0:T(8,128)(2,1)} %bitcast.11), calls=%async_computation.2 | async-start | bytes 458752 | tf_op jit(solution)/shard_map/all_to_all | solution.py:473
  64.5 7.1 %collective-permute-start.3 = (bf16[384,128]{1,0:T(8,128)(2,1)S(1)}, bf16[384,128]{1,0:T(8,128)(2,1)S(1)}, u32[]{:S(2)}, u32[]{:S(2)}) collective-permute-start(bf16[384,128]{1,0:T(8,128)(2,1)S(1)} %pad_maximum_fusion), channel_id=1, source_target_pairs={{0,1},{1,0},{2,3},{3,2},{4,5},{5,4},{6,7},{7,6},{8,9},{9,8},{10,11... | collective-permute-start | bytes 294920 | tf_op jit(solution)/shard_map/ppermute | solution.py:471
